TPU v7x, 32 devices: a whole 2x2x4 slice. The times are simulated.
32 devices in a mesh: lat: 4 (over y, x), lon: 8 (over z, core).
Axes of the slice: x: 2, y: 2, z: 4, core: 2. Of those that a mesh axis runs over, the one named last changes fastest.
Arguments:
- fields: bfloat16 [192, 256, 2, 256], P('lat', 'lon'), may hold values from -6 to 6
- ocean_mask: int32 [24, 32], P('lat'), may hold values from 0 to 1, as said below
- gain_one: float32 [256], replicated, may hold values from 0.1 to 1.9
- w_qkv: bfloat16 [256, 768], replicated, may hold values from -0.375 to 0.375
- rel_bias: float32 [8, 675], replicated, may hold values from -80 to 150
- w_proj: bfloat16 [256, 256], replicated, may hold values from -0.375 to 0.375
- gain_two: float32 [256], replicated, may hold values from 0.1 to 1.9
- w_up: bfloat16 [256, 1024], replicated, may hold values from -0.375 to 0.375
- w_down: bfloat16 [1024, 256], replicated, may hold values from -0.1875 to 0.1875
Outputs:
- ocean_out: bfloat16 [192, 256, 2, 256], P('lat', 'lon')
Inputs may be any that keep to these rules, and one draw needn't show every extreme that they name: `ocean_mask`: the windows of the last row of windows (a = 23) are land. Each band of 6 rows of windows held by one index of lat holds exactly 10 ocean windows per longitude device. Taking the devices of a band in order of longitude index, each holding 4 columns of windows, the ocean windows of the first d devices number at least d * 10 and at most d * 10 + 10; the upper bound is reached for some d in every band, at places drawn anew. One device holds 0 to 20 ocean windows.
All inputs are finite; a program needn't handle non-finite values.
Results may differ from a plain program's by a relative error of at most 0.0057.
Values may be sent and summed in bfloat16 or wider, within the bound.
A program may use at most 64 MiB of HBM per device.

v0:
```python
import math

import jax
import jax.numpy as jnp
from jax import lax
from jax.sharding import PartitionSpec as P

WIN_LAT = 8
WIN_LON = 8


NORM_FLOOR = 0.25


def shifted_2(array, axis, by):
    count = lax.axis_size(axis)
    pairs = [(i, i + by) for i in range(count) if 0 <= i + by < count]
    return lax.ppermute(array, axis, pairs)


def shifted_3(value, axis, steps):
    count = lax.axis_size(axis)
    pairs = [(source, (source + steps) % count) for source in range(count)]
    return lax.ppermute(value, axis, pairs)


def product(form, left, right):
    return jnp.einsum(form, left, right, preferred_element_type=jnp.float32)


def layer_norm(values, gain_vec):
    average = jnp.mean(values, axis=-1, keepdims=True)
    centred = values - average
    spread = jnp.mean(centred * centred, axis=-1, keepdims=True)
    return centred / jnp.sqrt(spread + NORM_FLOOR) * gain_vec


def bias_table(rel_bias, win_lat, win_lon, levels):
    tokens = win_lat * win_lon * levels
    token_ids = jnp.arange(tokens, dtype=jnp.int32)
    token_row = token_ids // (win_lon * levels)
    token_col = token_ids // levels % win_lon
    token_lev = token_ids % levels
    row_gap = token_row[:, None] - token_row[None, :] + win_lat - 1
    col_gap = token_col[:, None] - token_col[None, :] + win_lon - 1
    lev_gap = token_lev[:, None] - token_lev[None, :] + levels - 1
    lookup = (row_gap * (2 * win_lon - 1) + col_gap) * (2 * levels - 1) + lev_gap
    return jnp.take(rel_bias, lookup, axis=1)


def window_block(block, weights):
    gain_one, w_qkv, bias_full, w_proj, gain_two, w_up, w_down = weights
    window_count, tokens, features = block.shape
    head_count = bias_full.shape[0]
    head_dim = features // head_count
    score_scale = 1.0 / math.sqrt(head_dim)
    normed = layer_norm(block.astype(jnp.float32), gain_one).astype(jnp.bfloat16)
    triple = product("ntc,cf->ntf", normed, w_qkv).astype(jnp.bfloat16)
    triple = triple.reshape(window_count, tokens, 3, head_count, head_dim)
    query_part = triple[:, :, 0]
    key_part = triple[:, :, 1]
    value_part = triple[:, :, 2]
    scores = product("nthd,nshd->nhts", query_part, key_part) * score_scale + bias_full[None]
    row_top = jnp.max(scores, axis=-1, keepdims=True)
    exponent = jnp.exp(scores - row_top)
    attn_prob = (exponent / jnp.sum(exponent, axis=-1, keepdims=True)).astype(jnp.bfloat16)
    mixed = product("nhts,nshd->nthd", attn_prob, value_part).astype(jnp.bfloat16)
    mixed = mixed.reshape(window_count, tokens, features)
    middle = (block.astype(jnp.float32) + product("ntc,cf->ntf", mixed, w_proj)).astype(
        jnp.bfloat16
    )
    normed_two = layer_norm(middle.astype(jnp.float32), gain_two).astype(jnp.bfloat16)
    hidden = jax.nn.gelu(product("ntc,cf->ntf", normed_two, w_up), approximate=False).astype(
        jnp.bfloat16
    )
    return (middle.astype(jnp.float32) + product("ntf,fc->ntc", hidden, w_down)).astype(
        jnp.bfloat16
    )


def run_windows(windows, weights):
    total_rows = windows.shape[0]
    grouped = windows.reshape((total_rows // total_rows, total_rows) + windows.shape[1:])

    def one_group(group_win):
        return window_block(group_win, weights)

    finished = lax.map(one_group, grouped)
    return finished.reshape(windows.shape)


def pick_windows(grid, window_ids, lon_windows, features):
    row_ids = window_ids // lon_windows
    col_ids = window_ids % lon_windows
    taken = grid[row_ids, :, col_ids]
    return taken.reshape(window_ids.shape[0], -1, features)


def body(fields, ocean_mask, gain_one, w_qkv, rel_bias, w_proj, gain_two, w_up, w_down):
    lat_cells, lon_cells, levels, features = fields.shape
    lat_windows = lat_cells // WIN_LAT
    lon_windows = lon_cells // WIN_LON
    total_windows = lat_windows * lon_windows
    slot_count = (lat_windows - 1) * lon_windows // 2
    lat_half = WIN_LAT // 2
    lon_half = WIN_LON // 2
    north_strip = shifted_2(fields[:lat_half], "lat", -1)
    heightened = jnp.concatenate([fields[lat_half:], north_strip], axis=0)
    east_strip = shifted_3(heightened[:, :lon_half], "lon", -1)
    shifted = jnp.concatenate([heightened[:, lon_half:], east_strip], axis=1)
    row_width = WIN_LON * levels * features
    grid = shifted.reshape(lat_windows, WIN_LAT, lon_windows, row_width)
    bias_full = bias_table(rel_bias, WIN_LAT, WIN_LON, levels)
    weights = (gain_one, w_qkv, bias_full, w_proj, gain_two, w_up, w_down)
    cycle_size = lax.axis_size("lon")
    cycle_index = lax.axis_index("lon")
    per_device = jnp.sum(ocean_mask.reshape(lat_windows, cycle_size, lon_windows), axis=(0, 2))
    device_ids = jnp.arange(cycle_size, dtype=jnp.int32)
    before = jnp.sum(jnp.where(device_ids < cycle_index, per_device, 0))
    own_mask = lax.dynamic_slice_in_dim(
        ocean_mask, cycle_index * lon_windows, lon_windows, 1
    ).reshape(total_windows)
    own_count = jnp.sum(own_mask)
    window_ids = jnp.arange(total_windows, dtype=jnp.int32)
    ocean_order = jnp.argsort((1 - own_mask) * total_windows + window_ids)
    rank_ids = jnp.arange(2 * slot_count, dtype=jnp.int32)
    placed_ids = ocean_order[: 2 * slot_count]
    from_west = before - cycle_index * slot_count
    to_east = before + own_count - (cycle_index + 1) * slot_count
    kept_count = slot_count - from_west
    slot_ids = jnp.arange(slot_count, dtype=jnp.int32)
    own_pick = pick_windows(grid, ocean_order[:slot_count], lon_windows, features)
    send_from = jnp.clip(own_count - slot_count + slot_ids, 0, total_windows - 1)
    leaving = slot_ids >= slot_count - to_east
    outgoing = pick_windows(grid, ocean_order[send_from], lon_windows, features)
    outgoing = jnp.where(leaving[:, None, None], outgoing, jnp.zeros_like(outgoing))
    arriving = shifted_2(outgoing, "lon", 1)
    packed = jnp.where((slot_ids < kept_count)[:, None, None], own_pick, arriving)
    finished = run_windows(packed, weights)
    returned = shifted_2(finished, "lon", -1)
    pool_rows = jnp.concatenate([finished, returned], axis=0)
    source = jnp.where(
        rank_ids < kept_count, rank_ids, 2 * slot_count - to_east + rank_ids - kept_count
    )
    source = jnp.clip(source, 0, 2 * slot_count - 1)
    placed = jnp.take(pool_rows, source, axis=0)
    placed = jnp.where((rank_ids < own_count)[:, None, None], placed, jnp.zeros_like(placed))
    placed = placed.reshape(2 * slot_count, WIN_LAT, row_width)
    result = (
        jnp.zeros_like(grid).at[placed_ids // lon_windows, :, placed_ids % lon_windows].set(placed)
    )
    return result.reshape(lat_cells, lon_cells, levels, features)


def solution(mesh):
    in_specs = (P("lat", "lon", None, None), P("lat", None), P(), P(), P(), P(), P(), P(), P())
    out_specs = P("lat", "lon", None, None)
    return jax.shard_map(body, mesh=mesh, in_specs=in_specs, out_specs=out_specs, check_vma=False)
```

profile of v0, /device:TPU:3, one launch (start us, length us, event | category | flops | bytes accessed | tf_op | source)
XLA Modules:
  0.0 150.2 jit_solution(8831767497512915197)
XLA Ops:
  0.0 1.1 slice.32
  1.1 1.9 %collective-permute-start = (bf16[4,32,2,256]{3,2,1,0:T(2,128)(2,1)S(1)}, bf16[4,32,2,256]{3,2,1,0:T(2,128)(2,1)S(1)}, u32[]{:S(2)}, u32[]{:S(2)}) collective-permute-start(bf16[4,32,2,256]{3,2,1,0:T(2,128)(2,1)S(1)} %slice.32), channel_id=1, source_target_pairs={{8,0},{16,8},{24,16},{9,1},{17,9},{25,17},{10,2},{18,10},{26,18},{... | collective-permute-start | bytes 393224 | tf_op jit(solution)/shard_map/ppermute | solution.py:18
  3.0 0.7 reduce_sum.85
  3.7 1.4 dynamic-slice_reduce_fusion
  5.9 1.6 %sort.17 = (s32[24]{0:T(128)}, s32[24]{0:T(128)S(1)}) sort(s32[24]{0:T(128)S(1)} %iota_add_fusion, s32[24]{0:T(128)S(1)} %iota.64), dimensions={0}, to_apply=%region_0.1 | sort | flops 120 | bytes 384 | tf_op jit(solution)/shard_map/jit(argsort)/sort | solution.py:125
  7.5 0.7 gather_fusion.1
  10.5 2.6 %slice.31 = bf16[44,32,2,256]{3,2,1,0:T(2,128)(2,1)S(1)} slice(bf16[48,32,2,256]{3,2,1,0:T(2,128)(2,1)} %param.9), slice={[4:48], [0:32], [0:2], [0:256]} | slice | bytes 2883584 | tf_op jit(solution)/shard_map/slice | solution.py:108
  13.8 0.9 copy.32
  14.7 54.4 %gather_fusion.3 = f32[16384,8]{1,0:T(8,128)} fusion(f32[8,675]{0,1:T(8,128)S(1)} %copy.32, s32[16384]{0:T(1024)S(1)} %fusion.53), kind=kCustom, calls=%fused_computation.3 | custom fusion | bytes 1114112 | tf_op jit(solution)/shard_map/jit(_take)/gather | solution.py:48
  69.1 7.4 %copy.33 = f32[128,128,8]{0,1,2:T(8,128)} copy(f32[128,128,8]{2,1,0:T(8,128)} %bitcast.78) | data formatting | bytes 1048576 | tf_op jit(solution)/shard_map/jit(_take)/gather | solution.py:48
  76.8 0.7 collective-permute-start.1
  77.5 3.2 %fusion.24 = bf16[48,28,2,256]{3,2,1,0:T(2,128)(2,1)S(1)} fusion(bf16[44,32,2,256]{3,2,1,0:T(2,128)(2,1)S(1)} %slice.31, bf16[4,32,2,256]{3,2,1,0:T(2,128)(2,1)S(1)} %collective-permute-done), kind=kLoop, calls=%fused_computation.53 | loop fusion | flops 688128 | bytes 2949120 | tf_op jit(solution)/shard_map/concatenate | solution.py:108
  80.7 1.9 %collective-permute-done.1 = bf16[48,4,2,256]{3,2,1,0:T(2,128)(2,1)S(1)} collective-permute-done((bf16[48,4,2,256]{3,2,1,0:T(2,128)(2,1)S(1)}, bf16[48,4,2,256]{3,2,1,0:T(2,128)(2,1)S(1)}, u32[]{:S(2)}, u32[]{:S(2)}) %collective-permute-start.1) | collective-permute-done | bytes 196640 | tf_op jit(solution)/shard_map/ppermute | solution.py:24
  82.5 2.0 %pad_maximum_fusion = bf16[48,32,2,256]{3,2,1,0:T(2,128)(2,1)S(1)} fusion(bf16[48,4,2,256]{3,2,1,0:T(2,128)(2,1)S(1)} %collective-permute-done.1, bf16[48,28,2,256]{3,2,1,0:T(2,128)(2,1)S(1)} %fusion.24), kind=kLoop, calls=%fused_computation.48 | loop fusion | flops 786432 | bytes 3145728 | tf_op jit(solution)/shard_map/concatenate | solution.py:110
  84.6 2.3 %reshape.524 = bf16[6,8,4,4096]{3,2,1,0:T(4,128)(2,1)} reshape(bf16[48,32,2,256]{3,2,1,0:T(2,128)(2,1)S(1)} %pad_maximum_fusion) | data formatting | bytes 3145728 | tf_op jit(solution)/shard_map/reshape | solution.py:112
  86.8 2.3 %copy.26 = bf16[6,8,4,4096]{3,1,2,0:T(8,128)(2,1)S(1)} copy(bf16[6,8,4,4096]{3,2,1,0:T(4,128)(2,1)} %reshape.524) | data formatting | bytes 3145728 | tf_op jit(solution)/shard_map/reshape | solution.py:112
  90.1 1.0 broadcast_select_fusion
  91.0 2.1 %collective-permute-start.2 = (bf16[10,128,256]{2,1,0:T(8,128)(2,1)}, bf16[10,128,256]{2,1,0:T(8,128)(2,1)S(1)}, u32[]{:S(2)}, u32[]{:S(2)}) collective-permute-start(bf16[10,128,256]{2,1,0:T(8,128)(2,1)} %broadcast_select_fusion), channel_id=1, source_target_pairs={{0,1},{1,2},{2,3},{3,4},{4,5},{5,6},{6,7},{8,9},{9,10},{10,11},{11... | collective-permute-start | bytes 1966088 | tf_op jit(solution)/shard_map/ppermute | solution.py:18
  93.3 1.9 %select_bitcast_fusion = f32[8,128,128]{1,2,0:T(8,128)} fusion(f32[128,128,8]{0,1,2:T(8,128)} %copy.33, pred[128,128]{0,1:T(8,128)(4,1)S(1)} %compare_and_fusion), kind=kLoop, calls=%fused_computation.82 | loop fusion | flops 131072 | bytes 1064960 | tf_op jit(solution)/shard_map/jit(_take)/select_n | solution.py:48
  96.1 4.6 %collective-permute-done.2 = bf16[10,128,256]{2,1,0:T(8,128)(2,1)S(1)} collective-permute-done((bf16[10,128,256]{2,1,0:T(8,128)(2,1)}, bf16[10,128,256]{2,1,0:T(8,128)(2,1)S(1)}, u32[]{:S(2)}, u32[]{:S(2)}) %collective-permute-start.2) | collective-permute-done | bytes 655392 | tf_op jit(solution)/shard_map/ppermute | solution.py:18
  101.6 3.2 %convolution_convert_fusion = bf16[10,128,768]{2,1,0:T(8,128)(2,1)} fusion(bf16[10,128,256]{2,1,0:T(8,128)(2,1)S(1)} %get-tuple-element.28, f32[256]{0:T(256)S(1)} %copy-done.4, f32[10,128]{1,0:T(8,128)S(1)} %add_sqrt_fusion.1, f32[10,128]{1,0:T(8,128)S(1)} %broadcast_multiply_fusion.1, bf16[256,768]{1,0:T(8,128)(2,1)} %param.12), kind=kOutput, calls=%fused_computation.45 | convolution fusion | flops 505937920 | bytes 3025920 | tf_op jit(solution)/shard_map/while/body/eval_jaxpr/ntc,cf->ntf/dot_general | solution.py:28
  104.7 2.8 %copy.28 = bf16[10,128,768]{1,2,0:T(8,128)(2,1)S(1)} copy(bf16[10,128,768]{2,1,0:T(8,128)(2,1)} %convolution_convert_fusion) | data formatting | bytes 3932160 | tf_op jit(solution)/shard_map/while/body/eval_jaxpr/convert_element_type | solution.py:58
  107.6 0.9 fusion.41
  108.6 1.5 %fusion.107 = (f32[10,8,128]{2,1,0:T(8,128)S(1)}, f32[10,8,128,128]{2,3,1,0:T(8,128)S(1)}) fusion(f32[10,8,128,128]{2,3,1,0:T(8,128)S(1)} %fusion.41, f32[8,128,128]{1,2,0:T(8,128)S(1)} %copy-done.1), kind=kOutput, calls=%fused_computation.199 | output fusion | flops 7864447 | bytes 11051008 | tf_op jit(solution)/shard_map/while/body/eval_jaxpr/sub | solution.py:65
  110.2 0.8 fusion.26
  112.1 2.3 %fusion.14 = (u16[128,1024]{1,0:T(8,128)(2,1)S(1)}, u16[128,1024]{1,0:T(8,128)(2,1)S(1)}, f32[10,128,1024]{2,1,0:T(8,128)S(1)}) fusion(bf16[256,1024]{1,0:T(8,128)(2,1)S(1)} %copy-done, bf16[10,128,256]{2,1,0:T(8,128)(2,1)S(1)} %get-tuple-element.46, f32[256]{0:T(256)S(1)} %copy-done.5, f32[10,128]{1,0:T(8,128)S(1)} %add_sqrt_fusion, ...), kind=kOutput, calls=%fused_computation.36 | convolution fusion | flops 689504256 | bytes 6958080 | tf_op jit(solution)/shard_map/while/body/eval_jaxpr/ntc,cf->ntf/dot_general | solution.py:28
  114.4 12.8 %fusion.27 = bf16[10,128,256]{2,1,0:T(8,128)(2,1)S(1)} fusion(f32[10,128,1024]{2,1,0:T(8,128)S(1)} %get-tuple-element.47, bf16[10,128,256]{2,1,0:T(8,128)(2,1)S(1)} %get-tuple-element.46, u16[128,1024]{1,0:T(8,128)(2,1)S(1)} %get-tuple-element.26, u16[128,1024]{1,0:T(8,128)(2,1)S(1)} %get-tuple-element.25, bf16[1024,256]{1,0:T(8,128)(2,1)S(1)} %copy-done.3), kind=kOutput, calls=%fused_computation.56 | convolution fusion | flops 763822080 | bytes 7602176 | tf_op jit(solution)/shard_map/while/body/eval_jaxpr/ntf,fc->ntc/dot_general | solution.py:28
  127.2 2.2 %collective-permute-start.3 = (bf16[10,128,256]{2,1,0:T(8,128)(2,1)S(1)}, bf16[10,128,256]{2,1,0:T(8,128)(2,1)S(1)}, u32[]{:S(2)}, u32[]{:S(2)}) collective-permute-start(bf16[10,128,256]{2,1,0:T(8,128)(2,1)S(1)} %fusion.27), channel_id=1, source_target_pairs={{1,0},{2,1},{3,2},{4,3},{5,4},{6,5},{7,6},{9,8},{10,9},{11,10},{12... | collective-permute-start | bytes 1966088 | tf_op jit(solution)/shard_map/ppermute | solution.py:18
  130.1 9.7 %collective-permute-done.3 = bf16[10,128,256]{2,1,0:T(8,128)(2,1)S(1)} collective-permute-done((bf16[10,128,256]{2,1,0:T(8,128)(2,1)S(1)}, bf16[10,128,256]{2,1,0:T(8,128)(2,1)S(1)}, u32[]{:S(2)}, u32[]{:S(2)}) %collective-permute-start.3) | collective-permute-done | bytes 655392 | tf_op jit(solution)/shard_map/ppermute | solution.py:18
  141.6 2.0 %scatter_fusion = bf16[6,8,4,4096]{3,1,2,0:T(8,128)(2,1)S(1)} fusion(bf16[6,8,4,4096]{3,1,2,0:T(8,128)(2,1)S(1)} %broadcast_in_dim.100, s32[20]{0:T(128)S(1)} %fusion.74, bf16[20,8,4096]{2,1,0:T(8,128)(2,1)S(1)} %select_select_fusion), kind=kCustom, calls=%fused_computation.5 | custom fusion | bytes 3932320 | tf_op jit(solution)/shard_map/scatter | solution.py:150
  143.6 2.4 %copy.36 = bf16[6,8,4,4096]{3,2,1,0:T(4,128)(2,1)} copy(bf16[6,8,4,4096]{3,1,2,0:T(8,128)(2,1)S(1)} %scatter_fusion) | data formatting | bytes 3145728 | tf_op jit(solution)/shard_map/scatter | solution.py:150
  146.0 4.2 %reshape.529 = bf16[48,32,2,256]{3,2,1,0:T(2,128)(2,1)} reshape(bf16[6,8,4,4096]{3,2,1,0:T(4,128)(2,1)} %copy.36) | data formatting | bytes 3145728 | tf_op jit(solution)/shard_map/reshape | solution.py:152
  (52 shorter events, 7.8 us)
Async XLA Ops:
  0.0 112.0 %copy-start = (bf16[256,1024]{1,0:T(8,128)(2,1)S(1)}, bf16[256,1024]{1,0:T(8,128)(2,1)}, u32[]{:S(2)}) copy-start(bf16[256,1024]{1,0:T(8,128)(2,1)} %param.16) | copy-start | bytes 1572868
  1.1 75.4 %collective-permute-start = (bf16[4,32,2,256]{3,2,1,0:T(2,128)(2,1)S(1)}, bf16[4,32,2,256]{3,2,1,0:T(2,128)(2,1)S(1)}, u32[]{:S(2)}, u32[]{:S(2)}) collective-permute-start(bf16[4,32,2,256]{3,2,1,0:T(2,128)(2,1)S(1)} %slice.32), channel_id=1, source_target_pairs={{8,0},{16,8},{24,16},{9,1},{17,9},{25,17},{10,2},{18,10},{26,18},{... | collective-permute-start | bytes 393224 | tf_op jit(solution)/shard_map/ppermute | solution.py:18
  76.8 5.8 %collective-permute-start.1 = (bf16[48,4,2,256]{3,2,1,0:T(2,128)(2,1)S(1)}, bf16[48,4,2,256]{3,2,1,0:T(2,128)(2,1)S(1)}, u32[]{:S(2)}, u32[]{:S(2)}) collective-permute-start(bf16[48,4,2,256]{3,2,1,0:T(2,128)(2,1)S(1)} %pad_maximum_fusion.2), channel_id=1, source_target_pairs={{0,7},{1,0},{2,1},{3,2},{4,3},{5,4},{6,5},{7,6},{8,15},{9,8},{10,9... | collective-permute-start | bytes 589832 | tf_op jit(solution)/shard_map/ppermute | solution.py:24
  89.1 12.4 %copy-start.4 = (f32[256]{0:T(256)S(1)}, f32[256]{0:T(256)}, u32[]{:S(2)}) copy-start(f32[256]{0:T(256)} %param.11) | copy-start | bytes 3076
  91.0 9.7 %collective-permute-start.2 = (bf16[10,128,256]{2,1,0:T(8,128)(2,1)}, bf16[10,128,256]{2,1,0:T(8,128)(2,1)S(1)}, u32[]{:S(2)}, u32[]{:S(2)}) collective-permute-start(bf16[10,128,256]{2,1,0:T(8,128)(2,1)} %broadcast_select_fusion), channel_id=1, source_target_pairs={{0,1},{1,2},{2,3},{3,4},{4,5},{5,6},{6,7},{8,9},{9,10},{10,11},{11... | collective-permute-start | bytes 1966088 | tf_op jit(solution)/shard_map/ppermute | solution.py:18
  107.6 1.0 copy-start.1
  110.2 0.9 copy-start.2
  110.2 1.9 %copy-start.5 = (f32[256]{0:T(256)S(1)}, f32[256]{0:T(256)}, u32[]{:S(2)}) copy-start(f32[256]{0:T(256)} %param.15) | copy-start | bytes 3076
  112.1 2.3 %copy-start.3 = (bf16[1024,256]{1,0:T(8,128)(2,1)S(1)}, bf16[1024,256]{1,0:T(8,128)(2,1)}, u32[]{:S(2)}) copy-start(bf16[1024,256]{1,0:T(8,128)(2,1)} %param.17) | copy-start | bytes 1572868
  127.2 12.6 %collective-permute-start.3 = (bf16[10,128,256]{2,1,0:T(8,128)(2,1)S(1)}, bf16[10,128,256]{2,1,0:T(8,128)(2,1)S(1)}, u32[]{:S(2)}, u32[]{:S(2)}) collective-permute-start(bf16[10,128,256]{2,1,0:T(8,128)(2,1)S(1)} %fusion.27), channel_id=1, source_target_pairs={{1,0},{2,1},{3,2},{4,3},{5,4},{6,5},{7,6},{9,8},{10,9},{11,10},{12... | collective-permute-start | bytes 1966088 | tf_op jit(solution)/shard_map/ppermute | solution.py:18
where the time goes:
time: 152 us; the launch traced here: 150 us
  local copies, waits for them, and re-layouts  86.6 us (57%)
  matrix products  20.4 us (13%)
  other arithmetic  17 us (11%)
  waiting for transfers between devices  16.2 us (11%)
  starting transfers between devices  6.9 us (5%)
  between operations  2.99 us (2%)
    gather x2, local copies, waits for them, and re-layouts, bias_table(): return jnp.take(rel_bias, lookup, axis=1)  61.8 us
    dot_general x6, matrix products, product(): return jnp.einsum(form, left, right, preferred_element_type=jnp.float32)  20.4 us
    ppermute x3, waiting for transfers between devices, shifted_2(): return lax.ppermute(array, axis, pairs)  14.3 us
    ppermute x3, starting transfers between devices, shifted_2(): return lax.ppermute(array, axis, pairs)  6.18 us
    reshape x2, local copies, waits for them, and re-layouts, body(): grid = shifted.reshape(lat_windows, WIN_LAT, lon_windows, row_width)  4.56 us
    scatter x2, local copies, waits for them, and re-layouts, body(): jnp.zeros_like(grid)  4.38 us
    reshape x1, local copies, waits for them, and re-layouts, body(): return result.reshape(lat_cells, lon_cells, levels, features)  4.15 us
    concatenate x2, other arithmetic, body(): heightened = jnp.concatenate([fields[lat_half:], north_strip], axis=0)  3.43 us
  transfers between devices with their start and end apart: 4, of which 3 were waited for; matrix products, arithmetic and copies ran while one was open for 52% of the time, Pallas kernels for 0%

commit v1 on v0

v1 whole, which is shorter than its diff:
```python
import functools
import math

import jax
import jax.numpy as jnp
from jax import lax
from jax.experimental import pallas as pl
from jax.experimental.pallas import tpu as pltpu
from jax.sharding import PartitionSpec as P

WIN_LAT = 8
WIN_LON = 8
NORM_FLOOR = 0.25
LOG2E = math.log2(math.e)
ERF_COEFS = (1.1283793294596702, 0.10276689183983656, -0.0001854270054620651, -0.000625856981717449, 9.00024455627471e-05, -6.058558938836915e-06, 1.6416008301278458e-07)
ERF_LIMIT = 15.209999999999999


def bias_strips(rel_bias, levels):
    heads, length = rel_bias.shape
    col_step = 2 * levels - 1
    row_step = (2 * WIN_LON - 1) * col_step
    offsets = [c * col_step + lev for c in range(WIN_LON) for lev in range(levels)]
    top = offsets[-1]
    width = length - top
    scaled = rel_bias * LOG2E
    left = jnp.stack([scaled[:, top - q : top - q + width] for q in offsets], axis=1)
    group = WIN_LON * levels
    lane = jnp.arange(2 * WIN_LAT * group, dtype=jnp.int32)
    inner = lane % group
    target = lane // group * row_step + inner // levels * col_step + inner % levels
    pick = jnp.arange(width, dtype=jnp.int32)[:, None] == target[None, :]
    strips = jnp.dot(
        left.reshape(heads * group, width),
        pick.astype(jnp.float32),
        precision=lax.Precision.HIGHEST,
    )
    return strips.reshape(heads, group, 2 * WIN_LAT * group)


def gather_kernel(
    slots, half, mask_ref, where_ref, fields, north, east, corner, own, out_late, out_early, info, sems
):
    lat_windows = mask_ref.shape[0]
    lon_windows = fields.shape[1] // WIN_LON
    lat_half, lon_half = WIN_LAT // 2, WIN_LON // 2
    index = where_ref[0]
    first_col = index * lon_windows

    def count(col, total):
        for row in range(lat_windows):
            total = total + mask_ref[row, col]
        return total

    before = lax.fori_loop(0, first_col, count, jnp.int32(0))
    owned = lax.fori_loop(first_col, first_col + lon_windows, count, jnp.int32(0))
    kept = slots - (before - index * slots)
    to_east = before + owned - (index + 1) * slots
    info[0] = kept
    info[1] = slots - to_east - kept

    def fetch(row, col, window, block):
        low_lat, low_lon = row * WIN_LAT + lat_half, col * WIN_LON + lon_half
        last_row, last_col = row == lat_windows - 1, col == lon_windows - 1

        def quarter(source, down, right):
            target = block.at[pl.ds(down, lat_half), pl.ds(right, lon_half)]
            pltpu.make_async_copy(source, target, sems.at[window]).start()

        here = (pl.ds(low_lat, lat_half), pl.ds(low_lon, lon_half))
        quarter(fields.at[here[0], here[1]], 0, 0)

        @pl.when(jnp.logical_not(last_col))
        def _():
            quarter(fields.at[here[0], pl.ds(low_lon + lon_half, lon_half)], 0, lon_half)

        @pl.when(last_col)
        def _():
            quarter(east.at[here[0]], 0, lon_half)

        @pl.when(jnp.logical_not(last_row))
        def _():
            below = pl.ds(low_lat + lat_half, lat_half)
            quarter(fields.at[below, here[1]], lat_half, 0)

            @pl.when(jnp.logical_not(last_col))
            def _():
                quarter(fields.at[below, pl.ds(low_lon + lon_half, lon_half)], lat_half, lon_half)

            @pl.when(last_col)
            def _():
                quarter(east.at[below], lat_half, lon_half)

        @pl.when(last_row)
        def _():
            quarter(north.at[:, here[1]], lat_half, 0)

            @pl.when(jnp.logical_not(last_col))
            def _():
                quarter(north.at[:, pl.ds(low_lon + lon_half, lon_half)], lat_half, lon_half)

            @pl.when(last_col)
            def _():
                quarter(corner, lat_half, lon_half)

    def start(window, rank):
        row, col = window // lon_windows, window % lon_windows
        ocean = mask_ref[row, first_col + col]
        slot = slots - to_east + rank - kept

        @pl.when((ocean == 1) & (rank < kept))
        def _():
            fetch(row, col, window, own.at[rank])

        @pl.when((ocean == 1) & (rank >= kept) & (slot >= half))
        def _():
            fetch(row, col, window, out_late.at[slot - half])

        @pl.when((ocean == 1) & (rank >= kept) & (slot < half))
        def _():
            fetch(row, col, window, out_early.at[slot])

        return rank + ocean

    lax.fori_loop(0, lat_windows * lon_windows, start, jnp.int32(0))

    def finish(window, carry):
        row, col = window // lon_windows, window % lon_windows

        @pl.when(mask_ref[row, first_col + col] == 1)
        def _():
            block = fields.at[pl.ds(0, WIN_LAT), pl.ds(0, WIN_LON)]
            pltpu.make_async_copy(block, own.at[0], sems.at[window]).wait()

        return carry

    lax.fori_loop(0, lat_windows * lon_windows, finish, jnp.int32(0))


def place_kernel(
    half, mask_ref, where_ref, info, fin_early, fin_late, ret_early, ret_late, result, zero, sems
):
    lat_windows = mask_ref.shape[0]
    lon_windows = result.shape[1] // WIN_LON
    first_col = where_ref[0] * lon_windows
    zero[...] = jnp.zeros_like(zero)
    kept, ahead = info[0], info[1]

    def spot(window):
        row, col = window // lon_windows, window % lon_windows
        return result.at[pl.ds(row * WIN_LAT, WIN_LAT), pl.ds(col * WIN_LON, WIN_LON)]

    def start(window, rank):
        ocean = mask_ref[window // lon_windows, first_col + window % lon_windows]
        mine = rank < kept
        slot = jnp.where(mine, rank, rank + ahead)
        for pool, base, wanted, low in (
            (fin_early, 0, True, True),
            (fin_late, half, True, False),
            (ret_early, 0, False, True),
            (ret_late, half, False, False),
        ):
            side = mine if wanted else jnp.logical_not(mine)
            part = slot < half if low else slot >= half

            @pl.when((ocean == 1) & side & part)
            def _(pool=pool, base=base):
                pltpu.make_async_copy(
                    pool.at[slot - base], spot(window), sems.at[window]
                ).start()

        @pl.when(ocean == 0)
        def _():
            pltpu.make_async_copy(zero, spot(window), sems.at[window]).start()

        return rank + ocean

    lax.fori_loop(0, lat_windows * lon_windows, start, jnp.int32(0))

    def finish(window, carry):
        pltpu.make_async_copy(zero, spot(window), sems.at[window]).wait()
        return carry

    lax.fori_loop(0, lat_windows * lon_windows, finish, jnp.int32(0))


def normalise(values, gain):
    average = jnp.mean(values, axis=-1, keepdims=True)
    centred = values - average
    spread = jnp.mean(centred * centred, axis=-1, keepdims=True)
    return (centred * lax.rsqrt(spread + NORM_FLOOR) * gain).astype(jnp.bfloat16)


def erf_of(x):
    square = jnp.minimum(x * x, ERF_LIMIT)
    poly = jnp.full_like(square, ERF_COEFS[-1])
    for coef in ERF_COEFS[-2::-1]:
        poly = poly * square + coef
    return jnp.tanh(x * poly)


def dot(left, right):
    return jnp.dot(left, right, preferred_element_type=jnp.float32)


def window_kernel(
    base, info, own, arrived, strips, gain_one, w_qkv, w_proj, gain_two, w_up, w_down,
    out, bias, block, qkv, mixed,
):
    count = arrived.shape[0]
    heads, group, _ = strips.shape
    features = own.shape[-1]
    tokens = WIN_LAT * group
    dim = features // heads
    kept = info[0]
    scale = LOG2E / math.sqrt(dim)
    for row in range(WIN_LAT):
        first = (WIN_LAT - 1 - row) * group
        bias[:, row * group : (row + 1) * group, :] = strips[:, :, first : first + tokens]

    for n in range(count):
        slot = base + n

        @pl.when(slot < kept)
        def _():
            block[n * tokens : (n + 1) * tokens, :] = own[slot].reshape(tokens, features)

        @pl.when(slot >= kept)
        def _():
            block[n * tokens : (n + 1) * tokens, :] = arrived[n].reshape(tokens, features)

    values = block[...].astype(jnp.float32)
    normed = normalise(values, gain_one[...])
    qkv[...] = dot(normed, w_qkv[...]).astype(jnp.bfloat16)
    lane_head = lax.broadcasted_iota(jnp.int32, (tokens, features), 1) // dim

    def attend(n, carry):
        rows = pl.ds(pl.multiple_of(n * tokens, tokens), tokens)
        query_t = qkv[rows, :features].T
        key = qkv[rows, features : 2 * features]
        value_t = qkv[rows, 2 * features :].T
        parts = []
        for h in range(heads):
            masked = jnp.where(lane_head == h, key, jnp.zeros_like(key))
            scores = dot(masked, query_t) * scale + bias[h]
            power = jnp.exp2(scores - jnp.max(scores, axis=0, keepdims=True))
            total = jnp.sum(power, axis=0, keepdims=True)
            part = dot(value_t[h * dim : (h + 1) * dim, :], power.astype(jnp.bfloat16))
            parts.append((part * (1.0 / total)).astype(jnp.bfloat16))
        mixed[rows, :] = jnp.concatenate(parts, axis=0).T
        return carry

    lax.fori_loop(0, count, attend, 0, unroll=True)
    middle = (values + dot(mixed[...], w_proj[...])).astype(jnp.bfloat16)
    middle_wide = middle.astype(jnp.float32)
    normed_two = normalise(middle_wide, gain_two[...])
    total = middle_wide
    step = 256
    for k in range(w_up.shape[1] // step):
        cols = slice(k * step, (k + 1) * step)
        up = dot(normed_two, w_up[:, cols])
        grown = (0.5 * up * (1.0 + erf_of(up * math.sqrt(0.5)))).astype(jnp.bfloat16)
        total = total + dot(grown, w_down[cols, :])
    out[...] = total.astype(jnp.bfloat16).reshape(out.shape)


def vmem():
    return pl.BlockSpec(memory_space=pltpu.VMEM)


def smem():
    return pl.BlockSpec(memory_space=pltpu.SMEM)


def any_space():
    return pl.BlockSpec(memory_space=pl.ANY)


def cost(flops, moved):
    return pl.CostEstimate(flops=flops, bytes_accessed=moved, transcendentals=0)


def run_windows(base, info, own, arrived, strips, gain_one, w_qkv, w_proj, gain_two, w_up, w_down):
    count, _, _, levels, features = arrived.shape
    heads = strips.shape[0]
    tokens = WIN_LAT * WIN_LON * levels
    flops = 2 * count * tokens * features * (
        w_qkv.shape[1] + w_proj.shape[1] + 2 * w_up.shape[1] + 4 * tokens
    )
    return pl.pallas_call(
        functools.partial(window_kernel, base),
        out_shape=jax.ShapeDtypeStruct(arrived.shape, arrived.dtype),
        in_specs=[smem()] + [vmem()] * 9,
        out_specs=vmem(),
        scratch_shapes=[
            pltpu.VMEM((heads, tokens, tokens), jnp.float32),
            pltpu.VMEM((count * tokens, features), jnp.bfloat16),
            pltpu.VMEM((count * tokens, 3 * features), jnp.bfloat16),
            pltpu.VMEM((count * tokens, features), jnp.bfloat16),
        ],
        cost_estimate=cost(flops, 4 * arrived.size),
        compiler_params=pltpu.CompilerParams(vmem_limit_bytes=48 * 2**20),
    )(info, own, arrived, strips, gain_one, w_qkv, w_proj, gain_two, w_up, w_down)


def body(fields, ocean_mask, gain_one, w_qkv, rel_bias, w_proj, gain_two, w_up, w_down):
    lat_cells, lon_cells, levels, features = fields.shape
    lat_windows = lat_cells // WIN_LAT
    lon_windows = lon_cells // WIN_LON
    slots = (lat_windows - 1) * lon_windows // 2
    half = slots // 2
    late = slots - half
    lat_half, lon_half = WIN_LAT // 2, WIN_LON // 2
    lat_size, lon_size = lax.axis_size("lat"), lax.axis_size("lon")
    south = [(i, i - 1) for i in range(1, lat_size)]
    west = [(i, (i - 1) % lon_size) for i in range(lon_size)]
    diagonal = [
        (i * lon_size + j, (i - 1) * lon_size + (j - 1) % lon_size)
        for i in range(1, lat_size)
        for j in range(lon_size)
    ]
    onward = [(i, i + 1) for i in range(lon_size - 1)]
    backward = [(i + 1, i) for i in range(lon_size - 1)]
    east = lax.ppermute(fields[:, :lon_half], "lon", west)
    north = lax.ppermute(fields[:lat_half], "lat", south)
    corner = lax.ppermute(fields[:lat_half, :lon_half], ("lat", "lon"), diagonal)
    strips = bias_strips(rel_bias, levels)
    where = jnp.reshape(lax.axis_index("lon"), (1,)).astype(jnp.int32)
    shape = (WIN_LAT, WIN_LON, levels, features)
    window_count = lat_windows * lon_windows
    own, out_late, out_early, info = pl.pallas_call(
        functools.partial(gather_kernel, slots, half),
        out_shape=[
            jax.ShapeDtypeStruct((slots,) + shape, fields.dtype),
            jax.ShapeDtypeStruct((late,) + shape, fields.dtype),
            jax.ShapeDtypeStruct((half,) + shape, fields.dtype),
            jax.ShapeDtypeStruct((2,), jnp.int32),
        ],
        in_specs=[smem(), smem()] + [any_space()] * 4,
        out_specs=[vmem(), vmem(), vmem(), smem()],
        scratch_shapes=[pltpu.SemaphoreType.DMA((window_count,))],
        cost_estimate=cost(0, 4 * fields.size),
    )(ocean_mask, where, fields, north, east, corner)
    in_late = lax.ppermute(out_late, "lon", onward)
    in_early = lax.ppermute(out_early, "lon", onward)
    weights = (
        strips, gain_one.reshape(1, -1), w_qkv, w_proj, gain_two.reshape(1, -1), w_up, w_down,
    )
    fin_late = run_windows(half, info, own, in_late, *weights)
    ret_late = lax.ppermute(fin_late, "lon", backward)
    fin_early = run_windows(0, info, own, in_early, *weights)
    ret_early = lax.ppermute(fin_early, "lon", backward)
    return pl.pallas_call(
        functools.partial(place_kernel, half),
        out_shape=jax.ShapeDtypeStruct(fields.shape, fields.dtype),
        in_specs=[smem()] * 3 + [vmem()] * 4,
        out_specs=any_space(),
        scratch_shapes=[
            pltpu.VMEM(shape, fields.dtype),
            pltpu.SemaphoreType.DMA((window_count,)),
        ],
        cost_estimate=cost(0, 4 * fields.size),
    )(ocean_mask, where, info, fin_early, fin_late, ret_early, ret_late)


def solution(mesh):
    in_specs = (P("lat", "lon", None, None), P("lat", None), P(), P(), P(), P(), P(), P(), P())
    out_specs = P("lat", "lon", None, None)
    return jax.shard_map(body, mesh=mesh, in_specs=in_specs, out_specs=out_specs, check_vma=False)
```

time: 152 us -> 62.2 us (0.41)
  local copies, waits for them, and re-layouts: 86.6 us -> 7.22 us
  Pallas kernels: 0 us -> 25.8 us
  matrix products: 20.4 us -> 0.41 us
  other arithmetic: 17 us -> 0.75 us
  starting transfers between devices: 6.9 us -> 17.1 us
  waiting for transfers between devices: 16.2 us -> 9.04 us
  between operations: 2.99 us -> 0.57 us
    gather x7 -> x0, local copies, waits for them, and re-layouts: 64.9 us -> none  [the longest x2 61.8 us: bias_table(): return jnp.take(rel_bias, lookup, axis=1)]
    pallas_call x0 -> x4, Pallas kernels: none -> 25.8 us  [the longest x2 18.8 us: run_windows(): pl.pallas_call(functools.partial(window_kernel, base), out_shape=jax.Shap...]
    dot_general x6 -> x1, matrix products: 20.4 us -> 0.41 us  [bias_strips(): jnp.dot(left.reshape(heads * group, width), pick.astype(jnp.float32), pre...]
    ppermute x4 -> x7, starting transfers between devices: 6.9 us -> 17.1 us  [the longest x1 3.79 us: body(): in_early = lax.ppermute(out_early, 'lon', onward)]
    reshape x5 -> x0, local copies, waits for them, and re-layouts: 9.31 us -> none  [the longest x2 4.56 us: body(): grid = shifted.reshape(lat_windows, WIN_LAT, lon_windows, row_width)]
    ppermute x4 -> x7, waiting for transfers between devices: 16.2 us -> 9.04 us  [the longest x1 7.07 us: body(): ret_late = lax.ppermute(fin_late, 'lon', backward)]
    concatenate x7 -> x0, other arithmetic: 5.62 us -> none  [the longest x2 3.43 us: body(): heightened = jnp.concatenate([fields[lat_half:], north_strip], axis=0)]
    scatter x2 -> x0, local copies, waits for them, and re-layouts: 4.38 us -> none  [body(): jnp.zeros_like(grid)]
  transfers between devices with their start and end apart: 4 -> 7, of which waited for: 3 -> 2; matrix products, arithmetic and copies ran while one was open for 52% -> 7% of each run, Pallas kernels for 0% -> 31%
where the time goes in v1:
time: 62.2 us; the launch traced here: 61 us
  Pallas kernels  25.8 us (41%)
  starting transfers between devices  17.1 us (27%)
  waiting for transfers between devices  9.04 us (15%)
  local copies, waits for them, and re-layouts  7.22 us (12%)
  other arithmetic  0.75 us (1%)
    pallas_call x2, Pallas kernels, run_windows(): pl.pallas_call(functools.partial(window_kernel, base), out_shape=jax.Shap...  18.8 us
    ppermute x1, waiting for transfers between devices, body(): ret_late = lax.ppermute(fin_late, 'lon', backward)  7.07 us
    pallas_call x1, Pallas kernels, body(): pl.pallas_call(functools.partial(gather_kernel, slots, half), out_shape=[...  4.35 us
    ppermute x1, starting transfers between devices, body(): in_early = lax.ppermute(out_early, 'lon', onward)  3.79 us
    ppermute x1, starting transfers between devices, body(): east = lax.ppermute(fields[:, :lon_half], 'lon', west)  3.73 us
    unnamed x30, local copies, waits for them, and re-layouts  3.24 us
    pallas_call x1, Pallas kernels, body(): pl.pallas_call(functools.partial(place_kernel, half), out_shape=jax.Shape...  2.71 us
    ppermute x1, waiting for transfers between devices, body(): in_early = lax.ppermute(out_early, 'lon', onward)  1.95 us
  transfers between devices with their start and end apart: 7, of which 2 were waited for; matrix products, arithmetic and copies ran while one was open for 7% of the time, Pallas kernels for 31%

profile of v1, /device:TPU:3, one launch (start us, length us, event | category | flops | bytes accessed | tf_op | source)
XLA Modules:
  0.0 61.0 jit_solution(9102703282102844503)
XLA Ops:
  0.0 0.7 %slice.59 = bf16[4,4,2,256]{3,2,1,0:T(2,128)(2,1)S(1)} slice(bf16[48,32,2,256]{3,2,1,0:T(2,128)(2,1)} %fields.1), slice={[0:4], [0:4], [0:2], [0:256]} | slice | bytes 32768 | tf_op jit(solution)/shard_map/slice | solution.py:326
  0.7 1.9 %collective-permute-start.2 = (bf16[4,4,2,256]{3,2,1,0:T(2,128)(2,1)S(1)}, bf16[4,4,2,256]{3,2,1,0:T(2,128)(2,1)S(1)}, u32[]{:S(2)}, u32[]{:S(2)}) collective-permute-start(bf16[4,4,2,256]{3,2,1,0:T(2,128)(2,1)S(1)} %slice.59), channel_id=1, source_target_pairs={{8,7},{9,0},{10,1},{11,2},{12,3},{13,4},{14,5},{15,6},{16,15},{17,... | collective-permute-start | bytes 49160 | tf_op jit(solution)/shard_map/ppermute | solution.py:326
  2.7 1.0 %slice.57 = bf16[4,32,2,256]{3,2,1,0:T(2,128)(2,1)S(1)} slice(bf16[48,32,2,256]{3,2,1,0:T(2,128)(2,1)} %fields.1), slice={[0:4], [0:32], [0:2], [0:256]} | slice | bytes 262144 | tf_op jit(solution)/shard_map/slice | solution.py:325
  3.7 1.9 %collective-permute-start = (bf16[4,32,2,256]{3,2,1,0:T(2,128)(2,1)S(1)}, bf16[4,32,2,256]{3,2,1,0:T(2,128)(2,1)S(1)}, u32[]{:S(2)}, u32[]{:S(2)}) collective-permute-start(bf16[4,32,2,256]{3,2,1,0:T(2,128)(2,1)S(1)} %slice.57), channel_id=1, source_target_pairs={{8,0},{16,8},{24,16},{9,1},{17,9},{25,17},{10,2},{18,10},{26,18},{... | collective-permute-start | bytes 393224 | tf_op jit(solution)/shard_map/ppermute | solution.py:325
  5.6 1.1 %slice.58 = bf16[48,4,2,256]{3,2,1,0:T(2,128)(2,1)S(1)} slice(bf16[48,32,2,256]{3,2,1,0:T(2,128)(2,1)} %fields.1), slice={[0:48], [0:4], [0:2], [0:256]} | slice | bytes 393216 | tf_op jit(solution)/shard_map/slice | solution.py:324
  6.7 3.7 %collective-permute-start.1 = (bf16[48,4,2,256]{3,2,1,0:T(2,128)(2,1)S(1)}, bf16[48,4,2,256]{3,2,1,0:T(2,128)(2,1)S(1)}, u32[]{:S(2)}, u32[]{:S(2)}) collective-permute-start(bf16[48,4,2,256]{3,2,1,0:T(2,128)(2,1)S(1)} %slice.58), channel_id=1, source_target_pairs={{0,7},{1,0},{2,1},{3,2},{4,3},{5,4},{6,5},{7,6},{8,15},{9,8},{10,9... | collective-permute-start | bytes 589832 | tf_op jit(solution)/shard_map/ppermute | solution.py:324
  10.4 0.7 %broadcast_multiply_fusion = f32[8,675]{1,0:T(8,128)S(1)} fusion(f32[8,675]{1,0:T(8,128)} %param.13), kind=kLoop, calls=%fused_computation.19 | loop fusion | flops 5400 | bytes 43200 | tf_op jit(solution)/shard_map/mul | solution.py:26
  11.1 0.2 fusion.9
  11.9 0.0 copy-start.4
  11.9 0.0 copy-start.5
  11.9 0.0 copy-start.6
  11.9 0.0 copy-start.7
  11.9 0.0 copy-start.8
  11.9 0.0 copy-start.9
  11.9 0.6 stack.67
  12.6 0.5 copy-done.14
  13.2 0.1 copy-done.13
  13.2 0.1 copy-done.12
  13.3 4.3 %shard_map.91 = (bf16[10,8,8,2,256]{4,3,2,1,0:T(2,128)(2,1)}, bf16[5,8,8,2,256]{4,3,2,1,0:T(2,128)(2,1)}, bf16[5,8,8,2,256]{4,3,2,1,0:T(2,128)(2,1)}, s32[2]{0:T(128)}) custom-call(s32[6,32]{1,0:T(8,128)} %mask_ref.3, s32[1]{0:T(128)} %bitcast.where_ref, bf16[48,32,2,256]{3,2,1,0:T(2,128)(2,1)} %fields.1, bf16[4,32,2,256]{3,2,1,0:T(2,128)(2,1)} %copy-done.13, ...), custom_call_target="tpu_custom_call" | custom-call | bytes 3145728 | tf_op jit(solution)/shard_map/pallas_call | solution.py:331
  17.7 3.8 %collective-permute-start.3 = (bf16[5,8,8,2,256]{4,3,2,1,0:T(2,128)(2,1)}, bf16[5,8,8,2,256]{4,3,2,1,0:T(2,128)(2,1)S(1)}, u32[]{:S(2)}, u32[]{:S(2)}) collective-permute-start(bf16[5,8,8,2,256]{4,3,2,1,0:T(2,128)(2,1)} %get-tuple-element.11), channel_id=1, source_target_pairs={{0,1},{1,2},{2,3},{3,4},{4,5},{5,6},{6,7},{8,9},{9,10},{10,11},{11... | collective-permute-start | bytes 983048 | tf_op jit(solution)/shard_map/ppermute | solution.py:345
  21.5 1.9 %collective-permute-start.4 = (bf16[5,8,8,2,256]{4,3,2,1,0:T(2,128)(2,1)}, bf16[5,8,8,2,256]{4,3,2,1,0:T(2,128)(2,1)S(1)}, u32[]{:S(2)}, u32[]{:S(2)}) collective-permute-start(bf16[5,8,8,2,256]{4,3,2,1,0:T(2,128)(2,1)} %get-tuple-element.12), channel_id=1, source_target_pairs={{0,1},{1,2},{2,3},{3,4},{4,5},{5,6},{6,7},{8,9},{9,10},{10,11},{11... | collective-permute-start | bytes 983048 | tf_op jit(solution)/shard_map/ppermute | solution.py:344
  23.4 0.4 fusion.1.strips
  23.8 1.9 %collective-permute-done.3.arrived = bf16[5,8,8,2,256]{4,3,2,1,0:T(2,128)(2,1)S(1)} collective-permute-done((bf16[5,8,8,2,256]{4,3,2,1,0:T(2,128)(2,1)}, bf16[5,8,8,2,256]{4,3,2,1,0:T(2,128)(2,1)S(1)}, u32[]{:S(2)}, u32[]{:S(2)}) %collective-permute-start.3) | collective-permute-done | bytes 327712 | tf_op jit(solution)/shard_map/ppermute | solution.py:345
  25.8 0.7 %copy-done.2 = s32[2]{0:T(128)S(1)} copy-done((s32[2]{0:T(128)S(1)}, s32[2]{0:T(128)}, u32[]{:S(2)}) %copy-start.2) | copy-done | bytes 32
  26.5 1.1 %copy-done.3 = bf16[10,8,8,2,256]{4,3,2,1,0:T(2,128)(2,1)S(1)} copy-done((bf16[10,8,8,2,256]{4,3,2,1,0:T(2,128)(2,1)S(1)}, bf16[10,8,8,2,256]{4,3,2,1,0:T(2,128)(2,1)}, u32[]{:S(2)}) %copy-start.3) | copy-done | bytes 655384
  27.6 9.3 %shard_map.92.fin_early = bf16[5,8,8,2,256]{4,3,2,1,0:T(2,128)(2,1)S(1)} custom-call(s32[2]{0:T(128)S(1)} %copy-done.2, bf16[10,8,8,2,256]{4,3,2,1,0:T(2,128)(2,1)S(1)} %copy-done.3, bf16[5,8,8,2,256]{4,3,2,1,0:T(2,128)(2,1)S(1)} %collective-permute-done.3.arrived, f32[8,16,256]{2,1,0:T(8,128)S(1)} %fusion.1.strips, f32[1,256]{1,0:T(1,128)S(1)} %bitcast.37, ...), custom_call_target="tpu_custom_call" | custom-call | flops 1174405120 | bytes 655360 | tf_op jit(solution)/shard_map/pallas_call | solution.py:290
  36.9 1.9 %collective-permute-start.5 = (bf16[5,8,8,2,256]{4,3,2,1,0:T(2,128)(2,1)S(1)}, bf16[5,8,8,2,256]{4,3,2,1,0:T(2,128)(2,1)S(1)}, u32[]{:S(2)}, u32[]{:S(2)}) collective-permute-start(bf16[5,8,8,2,256]{4,3,2,1,0:T(2,128)(2,1)S(1)} %shard_map.92.fin_early), channel_id=1, source_target_pairs={{1,0},{2,1},{3,2},{4,3},{5,4},{6,5},{7,6},{9,8},{10,9},{11,10},{12... | collective-permute-start | bytes 983048 | tf_op jit(solution)/shard_map/ppermute | solution.py:352
  38.8 9.5 %shard_map.93.fin_late = bf16[5,8,8,2,256]{4,3,2,1,0:T(2,128)(2,1)S(1)} custom-call(s32[2]{0:T(128)S(1)} %copy-done.2, bf16[10,8,8,2,256]{4,3,2,1,0:T(2,128)(2,1)S(1)} %copy-done.3, bf16[5,8,8,2,256]{4,3,2,1,0:T(2,128)(2,1)S(1)} %collective-permute-done.4.arrived, f32[8,16,256]{2,1,0:T(8,128)S(1)} %fusion.1.strips, f32[1,256]{1,0:T(1,128)S(1)} %bitcast.38, ...), custom_call_target="tpu_custom_call" | custom-call | flops 1174405120 | bytes 655360 | tf_op jit(solution)/shard_map/pallas_call | solution.py:290
  48.3 1.9 %collective-permute-start.6 = (bf16[5,8,8,2,256]{4,3,2,1,0:T(2,128)(2,1)S(1)}, bf16[5,8,8,2,256]{4,3,2,1,0:T(2,128)(2,1)S(1)}, u32[]{:S(2)}, u32[]{:S(2)}) collective-permute-start(bf16[5,8,8,2,256]{4,3,2,1,0:T(2,128)(2,1)S(1)} %shard_map.93.fin_late), channel_id=1, source_target_pairs={{1,0},{2,1},{3,2},{4,3},{5,4},{6,5},{7,6},{9,8},{10,9},{11,10},{12... | collective-permute-start | bytes 983048 | tf_op jit(solution)/shard_map/ppermute | solution.py:350
  50.3 7.1 %collective-permute-done.6.ret_late = bf16[5,8,8,2,256]{4,3,2,1,0:T(2,128)(2,1)S(1)} collective-permute-done((bf16[5,8,8,2,256]{4,3,2,1,0:T(2,128)(2,1)S(1)}, bf16[5,8,8,2,256]{4,3,2,1,0:T(2,128)(2,1)S(1)}, u32[]{:S(2)}, u32[]{:S(2)}) %collective-permute-start.6) | collective-permute-done | bytes 327712 | tf_op jit(solution)/shard_map/ppermute | solution.py:350
  57.4 0.7 %copy-done.11 = bf16[5,8,8,2,256]{4,3,2,1,0:T(2,128)(2,1)} copy-done((bf16[5,8,8,2,256]{4,3,2,1,0:T(2,128)(2,1)}, bf16[5,8,8,2,256]{4,3,2,1,0:T(2,128)(2,1)S(1)}, u32[]{:S(2)}) %copy-start.11) | copy-done | bytes 327704
  58.1 2.7 %shard_map.94 = bf16[48,32,2,256]{3,2,1,0:T(2,128)(2,1)} custom-call(s32[6,32]{1,0:T(8,128)} %mask_ref.3, s32[1]{0:T(128)} %bitcast.where_ref, s32[2]{0:T(128)} %get-tuple-element.9.info, bf16[5,8,8,2,256]{4,3,2,1,0:T(2,128)(2,1)} %copy-done, bf16[5,8,8,2,256]{4,3,2,1,0:T(2,128)(2,1)} %copy-done.1, bf16[5,8,8,2,256]{4,3,2,1,0:T(2,128)(2,1)} %copy-done.10, ...), custom_call_target="tpu_custom_call" | custom-call | bytes 3145728 | tf_op jit(solution)/shard_map/pallas_call | solution.py:353
  (40 shorter events, 0.5 us)
Async XLA Ops:
  0.7 11.8 %collective-permute-start.2 = (bf16[4,4,2,256]{3,2,1,0:T(2,128)(2,1)S(1)}, bf16[4,4,2,256]{3,2,1,0:T(2,128)(2,1)S(1)}, u32[]{:S(2)}, u32[]{:S(2)}) collective-permute-start(bf16[4,4,2,256]{3,2,1,0:T(2,128)(2,1)S(1)} %slice.59), channel_id=1, source_target_pairs={{8,7},{9,0},{10,1},{11,2},{12,3},{13,4},{14,5},{15,6},{16,15},{17,... | collective-permute-start | bytes 49160 | tf_op jit(solution)/shard_map/ppermute | solution.py:326
  3.7 8.9 %collective-permute-start = (bf16[4,32,2,256]{3,2,1,0:T(2,128)(2,1)S(1)}, bf16[4,32,2,256]{3,2,1,0:T(2,128)(2,1)S(1)}, u32[]{:S(2)}, u32[]{:S(2)}) collective-permute-start(bf16[4,32,2,256]{3,2,1,0:T(2,128)(2,1)S(1)} %slice.57), channel_id=1, source_target_pairs={{8,0},{16,8},{24,16},{9,1},{17,9},{25,17},{10,2},{18,10},{26,18},{... | collective-permute-start | bytes 393224 | tf_op jit(solution)/shard_map/ppermute | solution.py:325
  6.7 5.9 %collective-permute-start.1 = (bf16[48,4,2,256]{3,2,1,0:T(2,128)(2,1)S(1)}, bf16[48,4,2,256]{3,2,1,0:T(2,128)(2,1)S(1)}, u32[]{:S(2)}, u32[]{:S(2)}) collective-permute-start(bf16[48,4,2,256]{3,2,1,0:T(2,128)(2,1)S(1)} %slice.58), channel_id=1, source_target_pairs={{0,7},{1,0},{2,1},{3,2},{4,3},{5,4},{6,5},{7,6},{8,15},{9,8},{10,9... | collective-permute-start | bytes 589832 | tf_op jit(solution)/shard_map/ppermute | solution.py:324
  11.9 13.9 %copy-start.4 = (bf16[256,1024]{1,0:T(8,128)(2,1)S(1)}, bf16[256,1024]{1,0:T(8,128)(2,1)}, u32[]{:S(2)}) copy-start(bf16[256,1024]{1,0:T(8,128)(2,1)} %w_up.3) | copy-start | bytes 1572868
  11.9 13.9 %copy-start.5 = (bf16[1024,256]{1,0:T(8,128)(2,1)S(1)}, bf16[1024,256]{1,0:T(8,128)(2,1)}, u32[]{:S(2)}) copy-start(bf16[1024,256]{1,0:T(8,128)(2,1)} %w_down.3) | copy-start | bytes 1572868
  11.9 13.9 %copy-start.6 = (bf16[256,768]{1,0:T(8,128)(2,1)S(1)}, bf16[256,768]{1,0:T(8,128)(2,1)}, u32[]{:S(2)}) copy-start(bf16[256,768]{1,0:T(8,128)(2,1)} %w_qkv.3) | copy-start | bytes 1179652
  11.9 13.9 %copy-start.7 = (bf16[256,256]{1,0:T(8,128)(2,1)S(1)}, bf16[256,256]{1,0:T(8,128)(2,1)}, u32[]{:S(2)}) copy-start(bf16[256,256]{1,0:T(8,128)(2,1)} %w_proj.3) | copy-start | bytes 393220
  11.9 13.9 %copy-start.8 = (f32[256]{0:T(256)S(1)}, f32[256]{0:T(256)}, u32[]{:S(2)}) copy-start(f32[256]{0:T(256)} %param.11) | copy-start | bytes 3076
  11.9 13.9 %copy-start.9 = (f32[256]{0:T(256)S(1)}, f32[256]{0:T(256)}, u32[]{:S(2)}) copy-start(f32[256]{0:T(256)} %param.15) | copy-start | bytes 3076
  12.5 0.6 copy-start.14
  12.6 0.6 %copy-start.13 = (bf16[4,32,2,256]{3,2,1,0:T(2,128)(2,1)}, bf16[4,32,2,256]{3,2,1,0:T(2,128)(2,1)S(1)}, u32[]{:S(2)}) copy-start(bf16[4,32,2,256]{3,2,1,0:T(2,128)(2,1)S(1)} %collective-permute-done.north) | copy-start | bytes 393220
  12.6 0.7 %copy-start.12 = (bf16[48,4,2,256]{3,2,1,0:T(2,128)(2,1)}, bf16[48,4,2,256]{3,2,1,0:T(2,128)(2,1)S(1)}, u32[]{:S(2)}) copy-start(bf16[48,4,2,256]{3,2,1,0:T(2,128)(2,1)S(1)} %collective-permute-done.1.east) | copy-start | bytes 589828
  17.7 8.1 %collective-permute-start.3 = (bf16[5,8,8,2,256]{4,3,2,1,0:T(2,128)(2,1)}, bf16[5,8,8,2,256]{4,3,2,1,0:T(2,128)(2,1)S(1)}, u32[]{:S(2)}, u32[]{:S(2)}) collective-permute-start(bf16[5,8,8,2,256]{4,3,2,1,0:T(2,128)(2,1)} %get-tuple-element.11), channel_id=1, source_target_pairs={{0,1},{1,2},{2,3},{3,4},{4,5},{5,6},{6,7},{8,9},{9,10},{10,11},{11... | collective-permute-start | bytes 983048 | tf_op jit(solution)/shard_map/ppermute | solution.py:345
  21.5 17.3 %collective-permute-start.4 = (bf16[5,8,8,2,256]{4,3,2,1,0:T(2,128)(2,1)}, bf16[5,8,8,2,256]{4,3,2,1,0:T(2,128)(2,1)S(1)}, u32[]{:S(2)}, u32[]{:S(2)}) collective-permute-start(bf16[5,8,8,2,256]{4,3,2,1,0:T(2,128)(2,1)} %get-tuple-element.12), channel_id=1, source_target_pairs={{0,1},{1,2},{2,3},{3,4},{4,5},{5,6},{6,7},{8,9},{9,10},{10,11},{11... | collective-permute-start | bytes 983048 | tf_op jit(solution)/shard_map/ppermute | solution.py:344
  25.8 0.7 %copy-start.2 = (s32[2]{0:T(128)S(1)}, s32[2]{0:T(128)}, u32[]{:S(2)}) copy-start(s32[2]{0:T(128)} %get-tuple-element.9.info) | copy-start | bytes 28
  26.5 1.1 %copy-start.3 = (bf16[10,8,8,2,256]{4,3,2,1,0:T(2,128)(2,1)S(1)}, bf16[10,8,8,2,256]{4,3,2,1,0:T(2,128)(2,1)}, u32[]{:S(2)}) copy-start(bf16[10,8,8,2,256]{4,3,2,1,0:T(2,128)(2,1)} %get-tuple-element.10.own) | copy-start | bytes 1966084
  36.9 11.4 %copy-start = (bf16[5,8,8,2,256]{4,3,2,1,0:T(2,128)(2,1)}, bf16[5,8,8,2,256]{4,3,2,1,0:T(2,128)(2,1)S(1)}, u32[]{:S(2)}) copy-start(bf16[5,8,8,2,256]{4,3,2,1,0:T(2,128)(2,1)S(1)} %shard_map.92.fin_early) | copy-start | bytes 983044
  36.9 13.4 %collective-permute-start.5 = (bf16[5,8,8,2,256]{4,3,2,1,0:T(2,128)(2,1)S(1)}, bf16[5,8,8,2,256]{4,3,2,1,0:T(2,128)(2,1)S(1)}, u32[]{:S(2)}, u32[]{:S(2)}) collective-permute-start(bf16[5,8,8,2,256]{4,3,2,1,0:T(2,128)(2,1)S(1)} %shard_map.92.fin_early), channel_id=1, source_target_pairs={{1,0},{2,1},{3,2},{4,3},{5,4},{6,5},{7,6},{9,8},{10,9},{11,10},{12... | collective-permute-start | bytes 983048 | tf_op jit(solution)/shard_map/ppermute | solution.py:352
  48.3 9.0 %copy-start.1 = (bf16[5,8,8,2,256]{4,3,2,1,0:T(2,128)(2,1)}, bf16[5,8,8,2,256]{4,3,2,1,0:T(2,128)(2,1)S(1)}, u32[]{:S(2)}) copy-start(bf16[5,8,8,2,256]{4,3,2,1,0:T(2,128)(2,1)S(1)} %shard_map.93.fin_late) | copy-start | bytes 983044
  48.3 9.0 %collective-permute-start.6 = (bf16[5,8,8,2,256]{4,3,2,1,0:T(2,128)(2,1)S(1)}, bf16[5,8,8,2,256]{4,3,2,1,0:T(2,128)(2,1)S(1)}, u32[]{:S(2)}, u32[]{:S(2)}) collective-permute-start(bf16[5,8,8,2,256]{4,3,2,1,0:T(2,128)(2,1)S(1)} %shard_map.93.fin_late), channel_id=1, source_target_pairs={{1,0},{2,1},{3,2},{4,3},{5,4},{6,5},{7,6},{9,8},{10,9},{11,10},{12... | collective-permute-start | bytes 983048 | tf_op jit(solution)/shard_map/ppermute | solution.py:350
  50.3 7.1 %copy-start.10 = (bf16[5,8,8,2,256]{4,3,2,1,0:T(2,128)(2,1)}, bf16[5,8,8,2,256]{4,3,2,1,0:T(2,128)(2,1)S(1)}, u32[]{:S(2)}) copy-start(bf16[5,8,8,2,256]{4,3,2,1,0:T(2,128)(2,1)S(1)} %collective-permute-done.5.ret_early) | copy-start | bytes 983044
  57.3 0.7 %copy-start.11 = (bf16[5,8,8,2,256]{4,3,2,1,0:T(2,128)(2,1)}, bf16[5,8,8,2,256]{4,3,2,1,0:T(2,128)(2,1)S(1)}, u32[]{:S(2)}) copy-start(bf16[5,8,8,2,256]{4,3,2,1,0:T(2,128)(2,1)S(1)} %collective-permute-done.6.ret_late) | copy-start | bytes 983044

commit v2 on v1

v2 whole, which is shorter than its diff:
```python
import functools
import math

import jax
import jax.numpy as jnp
from jax import lax
from jax.experimental import pallas as pl
from jax.experimental.pallas import tpu as pltpu
from jax.sharding import PartitionSpec as P

WIN_LAT = 8
WIN_LON = 8
NORM_FLOOR = 0.25
MESH = pl.DeviceIdType.MESH
LOG2E = math.log2(math.e)
ERF_COEFS = (1.1283793294596702, 0.10276689183983656, -0.0001854270054620651, -0.000625856981717449, 9.00024455627471e-05, -6.058558938836915e-06, 1.6416008301278458e-07)
ERF_LIMIT = 15.209999999999999


def bias_strips(rel_bias, levels):
    heads, length = rel_bias.shape
    col_step = 2 * levels - 1
    row_step = (2 * WIN_LON - 1) * col_step
    offsets = [c * col_step + lev for c in range(WIN_LON) for lev in range(levels)]
    top = offsets[-1]
    width = length - top
    scaled = rel_bias * LOG2E
    left = jnp.stack([scaled[:, top - q : top - q + width] for q in offsets], axis=1)
    group = WIN_LON * levels
    lane = jnp.arange(2 * WIN_LAT * group, dtype=jnp.int32)
    inner = lane % group
    target = lane // group * row_step + inner // levels * col_step + inner % levels
    pick = jnp.arange(width, dtype=jnp.int32)[:, None] == target[None, :]
    strips = jnp.dot(
        left.reshape(heads * group, width),
        pick.astype(jnp.float32),
        precision=lax.Precision.HIGHEST,
    )
    return strips.reshape(heads, group, 2 * WIN_LAT * group)


def halo_kernel(fields, north, east, corner, send_sems, recv_sems):
    lat_half, lon_half = WIN_LAT // 2, WIN_LON // 2
    lat, lon = lax.axis_index("lat"), lax.axis_index("lon")
    lat_size, lon_size = lax.axis_size("lat"), lax.axis_size("lon")
    west, east_of = (lon + lon_size - 1) % lon_size, (lon + 1) % lon_size
    barrier = pltpu.get_barrier_semaphore()

    def greet(row, col):
        pl.semaphore_signal(barrier, inc=1, device_id=(row, col), device_id_type=MESH)

    greet(lat, east_of)

    @pl.when(lat < lat_size - 1)
    def _():
        greet(lat + 1, lon)
        greet(lat + 1, east_of)

    def transfer(which, source, target, row, col):
        return pltpu.make_async_remote_copy(
            src_ref=source,
            dst_ref=target,
            send_sem=send_sems.at[which],
            recv_sem=recv_sems.at[which],
            device_id=(row, col),
            device_id_type=MESH,
        )

    up = jnp.maximum(lat - 1, 0)
    to_west = transfer(0, fields.at[:, pl.ds(0, lon_half)], east, lat, west)
    to_north = transfer(1, fields.at[pl.ds(0, lat_half)], north, up, lon)
    to_corner = transfer(
        2, fields.at[pl.ds(0, lat_half), pl.ds(0, lon_half)], corner, up, west
    )

    @pl.when(lat > 0)
    def _():
        pl.semaphore_wait(barrier, 3)
        to_north.start()
        to_corner.start()

    @pl.when(lat == 0)
    def _():
        pl.semaphore_wait(barrier, 1)

    to_west.start()
    to_west.wait()

    @pl.when(lat > 0)
    def _():
        to_north.wait_send()
        to_corner.wait_send()

    @pl.when(lat < lat_size - 1)
    def _():
        to_north.wait_recv()
        to_corner.wait_recv()


def gather_kernel(
    slots, mask_ref, where_ref, fields, north, east, corner, own, leaving, info, sems
):
    lat_windows = mask_ref.shape[0]
    lon_windows = fields.shape[1] // WIN_LON
    lat_half, lon_half = WIN_LAT // 2, WIN_LON // 2
    index = where_ref[0]
    first_col = index * lon_windows

    def count(col, total):
        for row in range(lat_windows):
            total = total + mask_ref[row, col]
        return total

    before = lax.fori_loop(0, first_col, count, jnp.int32(0))
    owned = lax.fori_loop(first_col, first_col + lon_windows, count, jnp.int32(0))
    kept = slots - (before - index * slots)
    to_east = before + owned - (index + 1) * slots
    info[0] = kept
    info[1] = slots - to_east - kept

    def fetch(row, col, window, block):
        low_lat, low_lon = row * WIN_LAT + lat_half, col * WIN_LON + lon_half
        last_row, last_col = row == lat_windows - 1, col == lon_windows - 1

        def quarter(source, down, right):
            target = block.at[pl.ds(down, lat_half), pl.ds(right, lon_half)]
            pltpu.make_async_copy(source, target, sems.at[window]).start()

        here = (pl.ds(low_lat, lat_half), pl.ds(low_lon, lon_half))
        quarter(fields.at[here[0], here[1]], 0, 0)

        @pl.when(jnp.logical_not(last_col))
        def _():
            quarter(fields.at[here[0], pl.ds(low_lon + lon_half, lon_half)], 0, lon_half)

        @pl.when(last_col)
        def _():
            quarter(east.at[here[0]], 0, lon_half)

        @pl.when(jnp.logical_not(last_row))
        def _():
            below = pl.ds(low_lat + lat_half, lat_half)
            quarter(fields.at[below, here[1]], lat_half, 0)

            @pl.when(jnp.logical_not(last_col))
            def _():
                quarter(fields.at[below, pl.ds(low_lon + lon_half, lon_half)], lat_half, lon_half)

            @pl.when(last_col)
            def _():
                quarter(east.at[below], lat_half, lon_half)

        @pl.when(last_row)
        def _():
            quarter(north.at[:, here[1]], lat_half, 0)

            @pl.when(jnp.logical_not(last_col))
            def _():
                quarter(north.at[:, pl.ds(low_lon + lon_half, lon_half)], lat_half, lon_half)

            @pl.when(last_col)
            def _():
                quarter(corner, lat_half, lon_half)

    def start(window, rank):
        row, col = window // lon_windows, window % lon_windows
        ocean = mask_ref[row, first_col + col]
        slot = slots - to_east + rank - kept

        @pl.when((ocean == 1) & (rank < kept))
        def _():
            fetch(row, col, window, own.at[rank])

        @pl.when((ocean == 1) & (rank >= kept))
        def _():
            fetch(row, col, window, leaving.at[slot])

        return rank + ocean

    lax.fori_loop(0, lat_windows * lon_windows, start, jnp.int32(0))

    def finish(window, carry):
        row, col = window // lon_windows, window % lon_windows

        @pl.when(mask_ref[row, first_col + col] == 1)
        def _():
            block = fields.at[pl.ds(0, WIN_LAT), pl.ds(0, WIN_LON)]
            pltpu.make_async_copy(block, own.at[0], sems.at[window]).wait()

        return carry

    lax.fori_loop(0, lat_windows * lon_windows, finish, jnp.int32(0))


def place_kernel(
    mask_ref, where_ref, info, finished, returned, result, zero, sems
):
    lat_windows = mask_ref.shape[0]
    lon_windows = result.shape[1] // WIN_LON
    first_col = where_ref[0] * lon_windows
    zero[...] = jnp.zeros_like(zero)
    kept, ahead = info[0], info[1]

    def spot(window):
        row, col = window // lon_windows, window % lon_windows
        return result.at[pl.ds(row * WIN_LAT, WIN_LAT), pl.ds(col * WIN_LON, WIN_LON)]

    def start(window, rank):
        ocean = mask_ref[window // lon_windows, first_col + window % lon_windows]

        @pl.when((ocean == 1) & (rank < kept))
        def _():
            pltpu.make_async_copy(finished.at[rank], spot(window), sems.at[window]).start()

        @pl.when((ocean == 1) & (rank >= kept))
        def _():
            source = returned.at[rank + ahead]
            pltpu.make_async_copy(source, spot(window), sems.at[window]).start()

        @pl.when(ocean == 0)
        def _():
            pltpu.make_async_copy(zero, spot(window), sems.at[window]).start()

        return rank + ocean

    lax.fori_loop(0, lat_windows * lon_windows, start, jnp.int32(0))

    def finish(window, carry):
        pltpu.make_async_copy(zero, spot(window), sems.at[window]).wait()
        return carry

    lax.fori_loop(0, lat_windows * lon_windows, finish, jnp.int32(0))


def normalise(values, gain):
    average = jnp.mean(values, axis=-1, keepdims=True)
    centred = values - average
    spread = jnp.mean(centred * centred, axis=-1, keepdims=True)
    return (centred * lax.rsqrt(spread + NORM_FLOOR) * gain).astype(jnp.bfloat16)


def erf_of(x):
    square = jnp.minimum(x * x, ERF_LIMIT)
    poly = jnp.full_like(square, ERF_COEFS[-1])
    for coef in ERF_COEFS[-2::-1]:
        poly = poly * square + coef
    return jnp.tanh(x * poly)


def dot(left, right):
    return jnp.dot(left, right, preferred_element_type=jnp.float32)


def window_kernel(
    chunk, info, own, leaving, strips, gain_one, w_qkv, w_proj, gain_two, w_up, w_down,
    finished, returned, arrived, bias, block, qkv, mixed,
    out_send, out_recv, back_send, back_recv,
):
    slots = own.shape[0]
    steps = slots // chunk
    heads, group, _ = strips.shape
    features = own.shape[-1]
    tokens = WIN_LAT * group
    dim = features // heads
    kept = info[0]
    scale = LOG2E / math.sqrt(dim)
    lat, lon = lax.axis_index("lat"), lax.axis_index("lon")
    last = lax.axis_size("lon") - 1
    east, west = jnp.minimum(lon + 1, last), jnp.maximum(lon - 1, 0)
    barrier = pltpu.get_barrier_semaphore()

    @pl.when(lon < last)
    def _():
        pl.semaphore_signal(barrier, inc=1, device_id=(lat, east), device_id_type=MESH)

    @pl.when(lon > 0)
    def _():
        pl.semaphore_signal(barrier, inc=1, device_id=(lat, west), device_id_type=MESH)

    @pl.when((lon > 0) & (lon < last))
    def _():
        pl.semaphore_wait(barrier, 2)

    @pl.when((lon == 0) | (lon == last))
    def _():
        pl.semaphore_wait(barrier, 1)

    def part(step):
        return pl.ds((steps - 1 - step) * chunk, chunk)

    def outward(step):
        return pltpu.make_async_remote_copy(
            src_ref=leaving.at[part(step)],
            dst_ref=arrived.at[part(step)],
            send_sem=out_send.at[step],
            recv_sem=out_recv.at[step],
            device_id=(lat, east),
            device_id_type=MESH,
        )

    def homeward(step):
        return pltpu.make_async_remote_copy(
            src_ref=finished.at[part(step)],
            dst_ref=returned.at[part(step)],
            send_sem=back_send.at[step],
            recv_sem=back_recv.at[step],
            device_id=(lat, west),
            device_id_type=MESH,
        )

    @pl.when(lon < last)
    def _():
        for step in range(steps):
            outward(step).start()

    @pl.when(lon == 0)
    def _():
        arrived[...] = jnp.zeros_like(arrived)

    for row in range(WIN_LAT):
        first = (WIN_LAT - 1 - row) * group
        bias[:, row * group : (row + 1) * group, :] = strips[:, :, first : first + tokens]

    lane_head = lax.broadcasted_iota(jnp.int32, (tokens, features), 1) // dim

    def attend(n):
        rows = slice(n * tokens, (n + 1) * tokens)
        query_t = qkv[rows, :features].T
        key = qkv[rows, features : 2 * features]
        value_t = qkv[rows, 2 * features :].T
        masked = [jnp.where(lane_head == h, key, jnp.zeros_like(key)) for h in range(heads)]
        every = dot(jnp.concatenate(masked, axis=0), query_t)
        parts = []
        for h in range(heads):
            scores = every[h * tokens : (h + 1) * tokens] * scale + bias[h]
            power = jnp.exp2(scores - jnp.max(scores, axis=0, keepdims=True))
            total = jnp.sum(power, axis=0, keepdims=True)
            piece = dot(value_t[h * dim : (h + 1) * dim, :], power.astype(jnp.bfloat16))
            parts.append((piece * (1.0 / total)).astype(jnp.bfloat16))
        mixed[rows, :] = jnp.concatenate(parts, axis=0).T

    def compute(step, carry):
        @pl.when(lon > 0)
        def _():
            outward(step).wait_recv()

        base = (steps - 1 - step) * chunk
        for n in range(chunk):
            slot = base + n
            mine = own[slot].reshape(tokens, features)
            other = arrived[slot].reshape(tokens, features)
            block[n * tokens : (n + 1) * tokens, :] = jnp.where(slot < kept, mine, other)
        values = block[...].astype(jnp.float32)
        normed = normalise(values, gain_one[...])
        qkv[...] = dot(normed, w_qkv[...]).astype(jnp.bfloat16)
        for n in range(chunk):
            attend(n)
        middle = (values + dot(mixed[...], w_proj[...])).astype(jnp.bfloat16)
        middle_wide = middle.astype(jnp.float32)
        normed_two = normalise(middle_wide, gain_two[...])
        up = dot(normed_two, w_up[...])
        grown = (0.5 * up * (1.0 + erf_of(up * math.sqrt(0.5)))).astype(jnp.bfloat16)
        result = (middle_wide + dot(grown, w_down[...])).astype(jnp.bfloat16)
        finished[part(step)] = result.reshape((chunk,) + finished.shape[1:])

        @pl.when(lon > 0)
        def _():
            homeward(step).start()

        return carry

    lax.fori_loop(0, steps, compute, 0)

    @pl.when(lon < last)
    def _():
        for step in range(steps):
            outward(step).wait_send()
            homeward(step).wait_recv()

    @pl.when(lon > 0)
    def _():
        for step in range(steps):
            homeward(step).wait_send()


def vmem():
    return pl.BlockSpec(memory_space=pltpu.VMEM)


def smem():
    return pl.BlockSpec(memory_space=pltpu.SMEM)


def any_space():
    return pl.BlockSpec(memory_space=pl.ANY)


def cost(flops, moved):
    return pl.CostEstimate(flops=flops, bytes_accessed=moved, transcendentals=0)


def run_windows(info, own, leaving, strips, gain_one, w_qkv, w_proj, gain_two, w_up, w_down):
    slots, _, _, levels, features = own.shape
    chunk = 2 if slots % 2 == 0 else 1
    heads = strips.shape[0]
    tokens = WIN_LAT * WIN_LON * levels
    flops = 2 * slots * tokens * features * (
        w_qkv.shape[1] + w_proj.shape[1] + 2 * w_up.shape[1] + 4 * tokens
    )
    return pl.pallas_call(
        functools.partial(window_kernel, chunk),
        out_shape=[jax.ShapeDtypeStruct(own.shape, own.dtype)] * 2,
        in_specs=[smem()] + [vmem()] * 9,
        out_specs=[vmem()] * 2,
        scratch_shapes=[
            pltpu.VMEM(own.shape, own.dtype),
            pltpu.VMEM((heads, tokens, tokens), jnp.float32),
            pltpu.VMEM((chunk * tokens, features), jnp.bfloat16),
            pltpu.VMEM((chunk * tokens, 3 * features), jnp.bfloat16),
            pltpu.VMEM((chunk * tokens, features), jnp.bfloat16),
        ]
        + [pltpu.SemaphoreType.DMA((slots // chunk,))] * 4,
        cost_estimate=cost(flops, 4 * own.size),
        compiler_params=pltpu.CompilerParams(
            collective_id=1, has_side_effects=True, vmem_limit_bytes=40 * 2**20
        ),
    )(info, own, leaving, strips, gain_one, w_qkv, w_proj, gain_two, w_up, w_down)


def exchange_halos(fields):
    lat_cells, lon_cells, levels, features = fields.shape
    lat_half, lon_half = WIN_LAT // 2, WIN_LON // 2
    return pl.pallas_call(
        halo_kernel,
        out_shape=[
            jax.ShapeDtypeStruct((lat_half, lon_cells, levels, features), fields.dtype),
            jax.ShapeDtypeStruct((lat_cells, lon_half, levels, features), fields.dtype),
            jax.ShapeDtypeStruct((lat_half, lon_half, levels, features), fields.dtype),
        ],
        in_specs=[any_space()],
        out_specs=[any_space()] * 3,
        scratch_shapes=[pltpu.SemaphoreType.DMA((3,))] * 2,
        cost_estimate=cost(0, fields.size),
        compiler_params=pltpu.CompilerParams(
            collective_id=0, has_side_effects=True, vmem_limit_bytes=2**20
        ),
    )(fields)


def body(fields, ocean_mask, gain_one, w_qkv, rel_bias, w_proj, gain_two, w_up, w_down):
    lat_cells, lon_cells, levels, features = fields.shape
    lat_windows = lat_cells // WIN_LAT
    lon_windows = lon_cells // WIN_LON
    slots = (lat_windows - 1) * lon_windows // 2
    north, east, corner = exchange_halos(fields)
    strips = bias_strips(rel_bias, levels)
    where = jnp.reshape(lax.axis_index("lon"), (1,)).astype(jnp.int32)
    shape = (WIN_LAT, WIN_LON, levels, features)
    window_count = lat_windows * lon_windows
    own, leaving, info = pl.pallas_call(
        functools.partial(gather_kernel, slots),
        out_shape=[
            jax.ShapeDtypeStruct((slots,) + shape, fields.dtype),
            jax.ShapeDtypeStruct((slots,) + shape, fields.dtype),
            jax.ShapeDtypeStruct((2,), jnp.int32),
        ],
        in_specs=[smem(), smem()] + [any_space()] * 4,
        out_specs=[vmem(), vmem(), smem()],
        scratch_shapes=[pltpu.SemaphoreType.DMA((window_count,))],
        cost_estimate=cost(0, 4 * fields.size),
        compiler_params=pltpu.CompilerParams(vmem_limit_bytes=3 * 2**20),
    )(ocean_mask, where, fields, north, east, corner)
    finished, returned = run_windows(
        info, own, leaving, strips, gain_one.reshape(1, -1), w_qkv, w_proj,
        gain_two.reshape(1, -1), w_up, w_down,
    )
    return pl.pallas_call(
        place_kernel,
        out_shape=jax.ShapeDtypeStruct(fields.shape, fields.dtype),
        in_specs=[smem()] * 3 + [any_space()] * 2,
        out_specs=any_space(),
        scratch_shapes=[
            pltpu.VMEM(shape, fields.dtype),
            pltpu.SemaphoreType.DMA((window_count,)),
        ],
        cost_estimate=cost(0, 4 * fields.size),
        compiler_params=pltpu.CompilerParams(vmem_limit_bytes=2**20),
    )(ocean_mask, where, info, finished, returned)


def solution(mesh):
    in_specs = (P("lat", "lon", None, None), P("lat", None), P(), P(), P(), P(), P(), P(), P())
    out_specs = P("lat", "lon", None, None)
    return jax.shard_map(body, mesh=mesh, in_specs=in_specs, out_specs=out_specs, check_vma=False)
```

time: 62.2 us -> 52.5 us (0.84); the launches traced: 61 us -> 51.9 us
  starting transfers between devices: 17.1 us -> 0 us
  Pallas kernels: 25.8 us -> 35.4 us
  waiting for transfers between devices: 9.04 us -> 0 us
  local copies, waits for them, and re-layouts: 7.22 us -> 14.1 us
  matrix products: 0.41 us -> 1.4 us
    ppermute x7 -> x0, starting transfers between devices: 17.1 us -> none  [the longest x1 3.79 us: body(): in_early = lax.ppermute(out_early, 'lon', onward)]
    another operation x17, local copies, waits for them, and re-layouts: 1.02 us -> 12.5 us  [bias_strips(): jnp.stack([scaled[:, top - q:top - q + width] for q in offsets], axis=1)]
    pallas_call x4, Pallas kernels: 25.8 us -> 35.4 us  [the longest x1 24.5 us: run_windows(): pl.pallas_call(functools.partial(window_kernel, chunk), out_shape=[jax.Sh...]
    ppermute x7 -> x0, waiting for transfers between devices: 9.04 us -> none  [the longest x1 7.07 us: body(): ret_late = lax.ppermute(fin_late, 'lon', backward)]
    slice x3 -> x0, local copies, waits for them, and re-layouts: 2.8 us -> none  [the longest x1 1.07 us: body(): east = lax.ppermute(fields[:, :lon_half], 'lon', west)]
    unnamed x30 -> x18, local copies, waits for them, and re-layouts: 3.24 us -> 1.45 us
    dot_general x1, matrix products: 0.41 us -> 1.4 us  [bias_strips(): jnp.dot(left.reshape(heads * group, width), pick.astype(jnp.float32), pre...]
  transfers between devices with their start and end apart: 7 -> 0, of which waited for: 2 -> 0; matrix products, arithmetic and copies ran while one was open for 7% -> 0% of each run, Pallas kernels for 31% -> 0%
where the time goes in v2:
time: 52.5 us; the launch traced here: 51.9 us
  Pallas kernels  35.4 us (67%)
  local copies, waits for them, and re-layouts  14.1 us (27%)
  matrix products  1.4 us (3%)
  other arithmetic  0.75 us (1%)
    pallas_call x1, Pallas kernels, run_windows(): pl.pallas_call(functools.partial(window_kernel, chunk), out_shape=[jax.Sh...  24.5 us
    another operation x17, local copies, waits for them, and re-layouts, bias_strips(): jnp.stack([scaled[:, top - q:top - q + width] for q in offsets], axis=1)  12.5 us
    pallas_call x1, Pallas kernels, exchange_halos(): pl.pallas_call(halo_kernel, out_shape=[jax.ShapeDtypeStruct((lat_half, lo...  5.98 us
    pallas_call x1, Pallas kernels, body(): pl.pallas_call(functools.partial(gather_kernel, slots), out_shape=[jax.Sh...  2.95 us
    pallas_call x1, Pallas kernels, body(): pl.pallas_call(place_kernel, out_shape=jax.ShapeDtypeStruct(fields.shape,...  1.96 us
    unnamed x18, local copies, waits for them, and re-layouts  1.45 us
    dot_general x1, matrix products, bias_strips(): jnp.dot(left.reshape(heads * group, width), pick.astype(jnp.float32), pre...  1.4 us

profile of v2, /device:TPU:3, one launch (start us, length us, event | category | flops | bytes accessed | tf_op | source)
XLA Modules:
  0.0 51.9 jit_solution(7671167379064780157)
XLA Ops:
  0.0 0.7 %broadcast_multiply_fusion = f32[8,675]{1,0:T(8,128)S(1)} fusion(f32[8,675]{1,0:T(8,128)} %param.13), kind=kLoop, calls=%fused_computation.19 | loop fusion | flops 5400 | bytes 43200 | tf_op jit(solution)/shard_map/mul | solution.py:27
  0.8 1.4 %copy-done = bf16[48,32,2,256]{3,2,1,0:T(2,128)(2,1)S(1)} copy-done((bf16[48,32,2,256]{3,2,1,0:T(2,128)(2,1)S(1)}, bf16[48,32,2,256]{3,2,1,0:T(2,128)(2,1)}, u32[]{:S(2)}) %copy-start) | copy-done | bytes 1572888
  2.2 6.0 %shard_map.91 = (bf16[4,32,2,256]{3,2,1,0:T(2,128)(2,1)S(1)}, bf16[48,4,2,256]{3,2,1,0:T(2,128)(2,1)S(1)}, bf16[4,4,2,256]{3,2,1,0:T(2,128)(2,1)S(1)}) custom-call(bf16[48,32,2,256]{3,2,1,0:T(2,128)(2,1)S(1)} %copy-done), custom_call_target="tpu_custom_call" | custom-call | bytes 786432 | tf_op jit(solution)/shard_map/pallas_call | solution.py:433
  8.1 0.0 copy-start.1
  8.2 0.0 copy-start.2
  8.2 0.2 fusion.9
  8.4 0.6 %copy.23 = f32[8,1,653]{2,1,0:T(1,128)} copy(f32[8,1,653]{2,0,1:T(8,128)S(1)} %get-tuple-element.23) | data formatting | bytes 41792 | tf_op jit(solution)/shard_map/stack | solution.py:28
  9.0 0.6 %copy.22 = f32[8,1,653]{2,1,0:T(1,128)} copy(f32[8,1,653]{2,0,1:T(8,128)S(1)} %get-tuple-element.24) | data formatting | bytes 41792 | tf_op jit(solution)/shard_map/stack | solution.py:28
  9.6 0.6 %copy.21 = f32[8,1,653]{2,1,0:T(1,128)} copy(f32[8,1,653]{2,0,1:T(8,128)S(1)} %get-tuple-element.25) | data formatting | bytes 41792 | tf_op jit(solution)/shard_map/stack | solution.py:28
  10.3 0.6 %copy.20 = f32[8,1,653]{2,1,0:T(1,128)} copy(f32[8,1,653]{2,0,1:T(8,128)S(1)} %get-tuple-element.26) | data formatting | bytes 41792 | tf_op jit(solution)/shard_map/stack | solution.py:28
  10.9 0.6 %copy.19 = f32[8,1,653]{2,1,0:T(1,128)} copy(f32[8,1,653]{2,0,1:T(8,128)S(1)} %get-tuple-element.27) | data formatting | bytes 41792 | tf_op jit(solution)/shard_map/stack | solution.py:28
  11.6 0.6 %copy.18 = f32[8,1,653]{2,1,0:T(1,128)} copy(f32[8,1,653]{2,0,1:T(8,128)S(1)} %get-tuple-element.28) | data formatting | bytes 41792 | tf_op jit(solution)/shard_map/stack | solution.py:28
  12.2 0.6 %copy.17 = f32[8,1,653]{2,1,0:T(1,128)} copy(f32[8,1,653]{2,0,1:T(8,128)S(1)} %get-tuple-element.29) | data formatting | bytes 41792 | tf_op jit(solution)/shard_map/stack | solution.py:28
  12.8 0.6 %copy.16 = f32[8,1,653]{2,1,0:T(1,128)} copy(f32[8,1,653]{2,0,1:T(8,128)S(1)} %get-tuple-element.30) | data formatting | bytes 41792 | tf_op jit(solution)/shard_map/stack | solution.py:28
  13.5 0.6 %copy.15 = f32[8,1,653]{2,1,0:T(1,128)} copy(f32[8,1,653]{2,0,1:T(8,128)S(1)} %get-tuple-element.31) | data formatting | bytes 41792 | tf_op jit(solution)/shard_map/stack | solution.py:28
  14.1 0.6 %copy.14 = f32[8,1,653]{2,1,0:T(1,128)} copy(f32[8,1,653]{2,0,1:T(8,128)S(1)} %get-tuple-element.32) | data formatting | bytes 41792 | tf_op jit(solution)/shard_map/stack | solution.py:28
  14.7 0.6 %copy.13 = f32[8,1,653]{2,1,0:T(1,128)} copy(f32[8,1,653]{2,0,1:T(8,128)S(1)} %get-tuple-element.33) | data formatting | bytes 41792 | tf_op jit(solution)/shard_map/stack | solution.py:28
  15.4 0.6 %copy.12 = f32[8,1,653]{2,1,0:T(1,128)} copy(f32[8,1,653]{2,0,1:T(8,128)S(1)} %get-tuple-element.34) | data formatting | bytes 41792 | tf_op jit(solution)/shard_map/stack | solution.py:28
  16.0 0.6 %copy.11 = f32[8,1,653]{2,1,0:T(1,128)} copy(f32[8,1,653]{2,0,1:T(8,128)S(1)} %get-tuple-element.35) | data formatting | bytes 41792 | tf_op jit(solution)/shard_map/stack | solution.py:28
  16.6 0.6 %copy.10 = f32[8,1,653]{2,1,0:T(1,128)} copy(f32[8,1,653]{2,0,1:T(8,128)S(1)} %get-tuple-element.36) | data formatting | bytes 41792 | tf_op jit(solution)/shard_map/stack | solution.py:28
  17.3 0.0 copy-start.7
  17.3 0.0 copy-start.8
  17.3 3.6 %stack.67 = f32[8,16,653]{2,1,0:T(8,128)} concatenate(f32[8,1,653]{2,1,0:T(1,128)} %copy.10, f32[8,1,653]{2,1,0:T(1,128)} %copy.11, f32[8,1,653]{2,1,0:T(1,128)} %copy.12, f32[8,1,653]{2,1,0:T(1,128)} %copy.13, f32[8,1,653]{2,1,0:T(1,128)} %copy.14, f32[8,1,653]{2,1,0:T(1,128)} %copy.15, f32[8,1,653]{2,1,0:T(1,128)} %copy.16, f32[8,1,653]{2,1,0:T(1,128)} %copy.17, ...), dimensions={1} | concatenate | bytes 668672 | tf_op jit(solution)/shard_map/stack | solution.py:28
  20.9 1.4 %fusion.1.strips = f32[8,16,256]{2,1,0:T(8,128)S(1)} fusion(f32[8,16,653]{2,1,0:T(8,128)} %stack.67, s32[256]{0:T(256)S(1)} %fusion.6), kind=kOutput, calls=%fused_computation.2 | convolution fusion | flops 256937216 | bytes 466432 | tf_op jit(solution)/shard_map/dot_general | solution.py:34
  22.3 0.0 copy-done.1
  22.4 0.0 copy-done.2
  22.4 2.9 %shard_map.92 = (bf16[10,8,8,2,256]{4,3,2,1,0:T(2,128)(2,1)S(1)}, bf16[10,8,8,2,256]{4,3,2,1,0:T(2,128)(2,1)S(1)}, s32[2]{0:T(128)S(1)}) custom-call(s32[6,32]{1,0:T(8,128)S(1)} %copy-done.2, s32[1]{0:T(128)} %bitcast.where_ref, bf16[48,32,2,256]{3,2,1,0:T(2,128)(2,1)S(1)} %copy-done.1, bf16[4,32,2,256]{3,2,1,0:T(2,128)(2,1)S(1)} %get-tuple-element.13.north, ...), custom_call_target="tpu_custom_call" | custom-call | bytes 3145728 | tf_op jit(solution)/shard_map/pallas_call | solution.py:460
  25.3 0.0 copy-done.3
  25.3 0.0 copy-done.4
  25.3 0.0 copy-done.5
  25.4 24.5 %shard_map.93 = (bf16[10,8,8,2,256]{4,3,2,1,0:T(2,128)(2,1)S(1)}, bf16[10,8,8,2,256]{4,3,2,1,0:T(2,128)(2,1)S(1)}) custom-call(s32[2]{0:T(128)S(1)} %get-tuple-element.16.info, bf16[10,8,8,2,256]{4,3,2,1,0:T(2,128)(2,1)S(1)} %get-tuple-element.17.own, bf16[10,8,8,2,256]{4,3,2,1,0:T(2,128)(2,1)S(1)} %get-tuple-element.18.leaving, ...), custom_call_target="tpu_custom_call" | custom-call | flops 2348810240 | bytes 1310720 | tf_op jit(solution)/shard_map/pallas_call | solution.py:410
  49.9 2.0 %shard_map.94 = bf16[48,32,2,256]{3,2,1,0:T(2,128)(2,1)} custom-call(s32[6,32]{1,0:T(8,128)S(1)} %copy-done.2, s32[1]{0:T(128)} %bitcast.where_ref, s32[2]{0:T(128)S(1)} %get-tuple-element.16.info, bf16[10,8,8,2,256]{4,3,2,1,0:T(2,128)(2,1)S(1)} %get-tuple-element.19.finished, bf16[10,8,8,2,256]{4,3,2,1,0:T(2,128)(2,1)S(1)} %get-tuple-element.20.returned), custom_call_target="tpu_custom_call" | custom-call | bytes 3145728 | tf_op jit(solution)/shard_map/pallas_call | solution.py:477
  (11 shorter events, 0.1 us)
Async XLA Ops:
  0.8 1.4 %copy-start = (bf16[48,32,2,256]{3,2,1,0:T(2,128)(2,1)S(1)}, bf16[48,32,2,256]{3,2,1,0:T(2,128)(2,1)}, u32[]{:S(2)}) copy-start(bf16[48,32,2,256]{3,2,1,0:T(2,128)(2,1)} %fields.3) | copy-start | bytes 4718596
  8.1 14.2 %copy-start.1 = (bf16[48,32,2,256]{3,2,1,0:T(2,128)(2,1)S(1)}, bf16[48,32,2,256]{3,2,1,0:T(2,128)(2,1)}, u32[]{:S(2)}) copy-start(bf16[48,32,2,256]{3,2,1,0:T(2,128)(2,1)} %fields.3) | copy-start | bytes 4718596
  8.2 14.2 %copy-start.2 = (s32[6,32]{1,0:T(8,128)S(1)}, s32[6,32]{1,0:T(8,128)}, u32[]{:S(2)}) copy-start(s32[6,32]{1,0:T(8,128)} %mask_ref.3) | copy-start | bytes 2308
  17.3 8.1 %copy-start.3 = (bf16[256,1024]{1,0:T(8,128)(2,1)S(1)}, bf16[256,1024]{1,0:T(8,128)(2,1)}, u32[]{:S(2)}) copy-start(bf16[256,1024]{1,0:T(8,128)(2,1)} %w_up.1) | copy-start | bytes 1572868
  17.3 8.1 %copy-start.4 = (bf16[1024,256]{1,0:T(8,128)(2,1)S(1)}, bf16[1024,256]{1,0:T(8,128)(2,1)}, u32[]{:S(2)}) copy-start(bf16[1024,256]{1,0:T(8,128)(2,1)} %w_down.1) | copy-start | bytes 1572868
  17.3 8.1 %copy-start.5 = (bf16[256,768]{1,0:T(8,128)(2,1)S(1)}, bf16[256,768]{1,0:T(8,128)(2,1)}, u32[]{:S(2)}) copy-start(bf16[256,768]{1,0:T(8,128)(2,1)} %w_qkv.1) | copy-start | bytes 1179652
  17.3 8.1 %copy-start.6 = (bf16[256,256]{1,0:T(8,128)(2,1)S(1)}, bf16[256,256]{1,0:T(8,128)(2,1)}, u32[]{:S(2)}) copy-start(bf16[256,256]{1,0:T(8,128)(2,1)} %w_proj.1) | copy-start | bytes 393220
  17.3 8.1 %copy-start.7 = (f32[256]{0:T(256)S(1)}, f32[256]{0:T(256)}, u32[]{:S(2)}) copy-start(f32[256]{0:T(256)} %param.11) | copy-start | bytes 3076
  17.3 8.1 %copy-start.8 = (f32[256]{0:T(256)S(1)}, f32[256]{0:T(256)}, u32[]{:S(2)}) copy-start(f32[256]{0:T(256)} %param.15) | copy-start | bytes 3076

commit v3 on v2

--- a/solution.py
+++ b/solution.py
@@ -17,29 +17,33 @@
 ERF_LIMIT = 15.209999999999999
 
 
-def bias_strips(rel_bias, levels):
+def bias_strips(rel_bias, padded, strips, levels):
     heads, length = rel_bias.shape
     col_step = 2 * levels - 1
     row_step = (2 * WIN_LON - 1) * col_step
     offsets = [c * col_step + lev for c in range(WIN_LON) for lev in range(levels)]
     top = offsets[-1]
-    width = length - top
-    scaled = rel_bias * LOG2E
-    left = jnp.stack([scaled[:, top - q : top - q + width] for q in offsets], axis=1)
+    width = padded.shape[1] - 128
+    padded[...] = jnp.zeros_like(padded)
+    padded[:, :length] = rel_bias[...] * LOG2E
+    table = padded[...]
+    left = jnp.concatenate([table[:, top - q : top - q + width] for q in offsets], axis=0)
     group = WIN_LON * levels
-    lane = jnp.arange(2 * WIN_LAT * group, dtype=jnp.int32)
+    lane = lax.broadcasted_iota(jnp.int32, (width, strips.shape[2]), 1)
     inner = lane % group
     target = lane // group * row_step + inner // levels * col_step + inner % levels
-    pick = jnp.arange(width, dtype=jnp.int32)[:, None] == target[None, :]
-    strips = jnp.dot(
-        left.reshape(heads * group, width),
+    pick = lax.broadcasted_iota(jnp.int32, target.shape, 0) == target
+    found = jnp.dot(
+        left,
         pick.astype(jnp.float32),
         precision=lax.Precision.HIGHEST,
+        preferred_element_type=jnp.float32,
     )
-    return strips.reshape(heads, group, 2 * WIN_LAT * group)
-
-
-def halo_kernel(fields, north, east, corner, send_sems, recv_sems):
+    for place in range(group):
+        strips[:, place, :] = found[place * heads : (place + 1) * heads]
+
+
+def halo_kernel(fields, rel_bias, north, east, corner, strips, padded, send_sems, recv_sems):
     lat_half, lon_half = WIN_LAT // 2, WIN_LON // 2
     lat, lon = lax.axis_index("lat"), lax.axis_index("lon")
     lat_size, lon_size = lax.axis_size("lat"), lax.axis_size("lon")
@@ -84,6 +88,7 @@
         pl.semaphore_wait(barrier, 1)
 
     to_west.start()
+    bias_strips(rel_bias, padded, strips, fields.shape[2])
     to_west.wait()
 
     @pl.when(lat > 0)
@@ -427,24 +432,28 @@
     )(info, own, leaving, strips, gain_one, w_qkv, w_proj, gain_two, w_up, w_down)
 
 
-def exchange_halos(fields):
+def exchange_halos(fields, rel_bias):
     lat_cells, lon_cells, levels, features = fields.shape
     lat_half, lon_half = WIN_LAT // 2, WIN_LON // 2
+    heads, length = rel_bias.shape
+    group = WIN_LON * levels
     return pl.pallas_call(
         halo_kernel,
         out_shape=[
             jax.ShapeDtypeStruct((lat_half, lon_cells, levels, features), fields.dtype),
             jax.ShapeDtypeStruct((lat_cells, lon_half, levels, features), fields.dtype),
             jax.ShapeDtypeStruct((lat_half, lon_half, levels, features), fields.dtype),
+            jax.ShapeDtypeStruct((heads, group, 2 * WIN_LAT * group), jnp.float32),
         ],
-        in_specs=[any_space()],
-        out_specs=[any_space()] * 3,
-        scratch_shapes=[pltpu.SemaphoreType.DMA((3,))] * 2,
+        in_specs=[pl.BlockSpec(memory_space=pltpu.HBM), vmem()],
+        out_specs=[any_space()] * 3 + [vmem()],
+        scratch_shapes=[pltpu.VMEM((heads, (length + 255) // 128 * 128), jnp.float32)]
+        + [pltpu.SemaphoreType.DMA((3,))] * 2,
         cost_estimate=cost(0, fields.size),
         compiler_params=pltpu.CompilerParams(
-            collective_id=0, has_side_effects=True, vmem_limit_bytes=2**20
+            collective_id=0, has_side_effects=True, vmem_limit_bytes=4 * 2**20
         ),
-    )(fields)
+    )(fields, rel_bias)
 
 
 def body(fields, ocean_mask, gain_one, w_qkv, rel_bias, w_proj, gain_two, w_up, w_down):
@@ -452,8 +461,7 @@
     lat_windows = lat_cells // WIN_LAT
     lon_windows = lon_cells // WIN_LON
     slots = (lat_windows - 1) * lon_windows // 2
-    north, east, corner = exchange_halos(fields)
-    strips = bias_strips(rel_bias, levels)
+    north, east, corner, strips = exchange_halos(fields, rel_bias)
     where = jnp.reshape(lax.axis_index("lon"), (1,)).astype(jnp.int32)
     shape = (WIN_LAT, WIN_LON, levels, features)
     window_count = lat_windows * lon_windows

time: 52.5 us -> 38.3 us (0.73)
  local copies, waits for them, and re-layouts: 14.1 us -> 2.19 us
  matrix products: 1.4 us -> 0 us
  other arithmetic: 0.75 us -> 0 us
    another operation x17 -> x0, local copies, waits for them, and re-layouts: 12.5 us -> none  [bias_strips(): jnp.stack([scaled[:, top - q:top - q + width] for q in offsets], axis=1)]
    dot_general x1 -> x0, matrix products: 1.4 us -> none  [bias_strips(): jnp.dot(left.reshape(heads * group, width), pick.astype(jnp.float32), pre...]
    mul x1 -> x0, other arithmetic: 0.74 us -> none  [bias_strips(): scaled = rel_bias * LOG2E]
    unnamed x18 -> x20, local copies, waits for them, and re-layouts: 1.45 us -> 2.19 us
where the time goes in v3:
time: 38.3 us; the launch traced here: 37.8 us
  Pallas kernels  35.5 us (93%)
  local copies, waits for them, and re-layouts  2.19 us (6%)
    pallas_call x1, Pallas kernels, run_windows(): pl.pallas_call(functools.partial(window_kernel, chunk), out_shape=[jax.Sh...  24.3 us
    pallas_call x1, Pallas kernels, exchange_halos(): pl.pallas_call(halo_kernel, out_shape=[jax.ShapeDtypeStruct((lat_half, lo...  6.02 us
    pallas_call x1, Pallas kernels, body(): pl.pallas_call(functools.partial(gather_kernel, slots), out_shape=[jax.Sh...  3.25 us
    unnamed x20, local copies, waits for them, and re-layouts  2.19 us
    pallas_call x1, Pallas kernels, body(): pl.pallas_call(place_kernel, out_shape=jax.ShapeDtypeStruct(fields.shape,...  1.96 us

profile of v3, /device:TPU:3, one launch (start us, length us, event | category | flops | bytes accessed | tf_op | source)
XLA Modules:
  0.0 37.8 jit_solution(18374188087301383290)
XLA Ops:
  0.0 0.0 copy-start.3
  0.0 0.0 copy-start
  0.0 1.4 %copy-done = bf16[48,32,2,256]{3,2,1,0:T(2,128)(2,1)S(1)} copy-done((bf16[48,32,2,256]{3,2,1,0:T(2,128)(2,1)S(1)}, bf16[48,32,2,256]{3,2,1,0:T(2,128)(2,1)}, u32[]{:S(2)}) %copy-start) | copy-done | bytes 1572888
  1.4 0.0 copy-start.2
  1.4 0.7 %copy-done.2 = f32[8,675]{1,0:T(8,128)S(1)} copy-done((f32[8,675]{1,0:T(8,128)S(1)}, f32[8,675]{1,0:T(8,128)}, u32[]{:S(2)}) %copy-start.2) | copy-done | bytes 21624
  2.2 0.0 copy-start.1
  2.2 0.0 copy-start.4
  2.2 0.0 copy-start.5
  2.2 0.0 copy-start.6
  2.2 0.0 copy-start.7
  2.2 0.0 copy-start.8
  2.2 0.0 copy-start.9
  2.2 6.0 %shard_map.91 = (bf16[4,32,2,256]{3,2,1,0:T(2,128)(2,1)S(1)}, bf16[48,4,2,256]{3,2,1,0:T(2,128)(2,1)S(1)}, bf16[4,4,2,256]{3,2,1,0:T(2,128)(2,1)S(1)}, f32[8,16,256]{2,1,0:T(8,128)S(1)}) custom-call(bf16[48,32,2,256]{3,2,1,0:T(2,128)(2,1)S(1)} %copy-done, f32[8,675]{1,0:T(8,128)S(1)} %copy-done.2), custom_call_target="tpu_custom_call" | custom-call | bytes 786432 | tf_op jit(solution)/shard_map/pallas_call | solution.py:440
  8.2 0.0 copy-done.3
  8.2 0.0 copy-done.1
  8.3 3.2 %shard_map.92 = (bf16[10,8,8,2,256]{4,3,2,1,0:T(2,128)(2,1)S(1)}, bf16[10,8,8,2,256]{4,3,2,1,0:T(2,128)(2,1)S(1)}, s32[2]{0:T(128)S(1)}) custom-call(s32[6,32]{1,0:T(8,128)S(1)} %copy-done.3, s32[1]{0:T(128)} %bitcast.where_ref, bf16[48,32,2,256]{3,2,1,0:T(2,128)(2,1)S(1)} %copy-done.1, bf16[4,32,2,256]{3,2,1,0:T(2,128)(2,1)S(1)} %get-tuple-element.14.north, ...), custom_call_target="tpu_custom_call" | custom-call | bytes 3145728 | tf_op jit(solution)/shard_map/pallas_call | solution.py:468
  11.5 0.0 copy-done.4
  11.5 0.0 copy-done.5
  11.5 0.0 copy-done.6
  11.5 0.0 copy-done.7
  11.6 0.0 copy-done.8
  11.6 0.0 copy-done.9
  11.6 24.3 %shard_map.93 = (bf16[10,8,8,2,256]{4,3,2,1,0:T(2,128)(2,1)S(1)}, bf16[10,8,8,2,256]{4,3,2,1,0:T(2,128)(2,1)S(1)}) custom-call(s32[2]{0:T(128)S(1)} %get-tuple-element.17.info, bf16[10,8,8,2,256]{4,3,2,1,0:T(2,128)(2,1)S(1)} %get-tuple-element.18.own, bf16[10,8,8,2,256]{4,3,2,1,0:T(2,128)(2,1)S(1)} %get-tuple-element.19.leaving, ...), custom_call_target="tpu_custom_call" | custom-call | flops 2348810240 | bytes 1310720 | tf_op jit(solution)/shard_map/pallas_call | solution.py:415
  35.9 2.0 %shard_map.94 = bf16[48,32,2,256]{3,2,1,0:T(2,128)(2,1)} custom-call(s32[6,32]{1,0:T(8,128)S(1)} %copy-done.3, s32[1]{0:T(128)} %bitcast.where_ref, s32[2]{0:T(128)S(1)} %get-tuple-element.17.info, bf16[10,8,8,2,256]{4,3,2,1,0:T(2,128)(2,1)S(1)} %get-tuple-element.21.finished, bf16[10,8,8,2,256]{4,3,2,1,0:T(2,128)(2,1)S(1)} %get-tuple-element.22.returned), custom_call_target="tpu_custom_call" | custom-call | bytes 3145728 | tf_op jit(solution)/shard_map/pallas_call | solution.py:485
Async XLA Ops:
  0.0 8.2 %copy-start.3 = (s32[6,32]{1,0:T(8,128)S(1)}, s32[6,32]{1,0:T(8,128)}, u32[]{:S(2)}) copy-start(s32[6,32]{1,0:T(8,128)} %mask_ref.3) | copy-start | bytes 2308
  0.0 1.4 %copy-start = (bf16[48,32,2,256]{3,2,1,0:T(2,128)(2,1)S(1)}, bf16[48,32,2,256]{3,2,1,0:T(2,128)(2,1)}, u32[]{:S(2)}) copy-start(bf16[48,32,2,256]{3,2,1,0:T(2,128)(2,1)} %fields.3) | copy-start | bytes 4718596
  1.4 0.7 %copy-start.2 = (f32[8,675]{1,0:T(8,128)S(1)}, f32[8,675]{1,0:T(8,128)}, u32[]{:S(2)}) copy-start(f32[8,675]{1,0:T(8,128)} %rel_bias.1) | copy-start | bytes 64804
  2.2 6.1 %copy-start.1 = (bf16[48,32,2,256]{3,2,1,0:T(2,128)(2,1)S(1)}, bf16[48,32,2,256]{3,2,1,0:T(2,128)(2,1)}, u32[]{:S(2)}) copy-start(bf16[48,32,2,256]{3,2,1,0:T(2,128)(2,1)} %fields.3) | copy-start | bytes 4718596
  2.2 9.4 %copy-start.4 = (bf16[256,1024]{1,0:T(8,128)(2,1)S(1)}, bf16[256,1024]{1,0:T(8,128)(2,1)}, u32[]{:S(2)}) copy-start(bf16[256,1024]{1,0:T(8,128)(2,1)} %w_up.1) | copy-start | bytes 1572868
  2.2 9.4 %copy-start.5 = (bf16[1024,256]{1,0:T(8,128)(2,1)S(1)}, bf16[1024,256]{1,0:T(8,128)(2,1)}, u32[]{:S(2)}) copy-start(bf16[1024,256]{1,0:T(8,128)(2,1)} %w_down.1) | copy-start | bytes 1572868
  2.2 9.4 %copy-start.6 = (bf16[256,768]{1,0:T(8,128)(2,1)S(1)}, bf16[256,768]{1,0:T(8,128)(2,1)}, u32[]{:S(2)}) copy-start(bf16[256,768]{1,0:T(8,128)(2,1)} %w_qkv.1) | copy-start | bytes 1179652
  2.2 9.4 %copy-start.7 = (bf16[256,256]{1,0:T(8,128)(2,1)S(1)}, bf16[256,256]{1,0:T(8,128)(2,1)}, u32[]{:S(2)}) copy-start(bf16[256,256]{1,0:T(8,128)(2,1)} %w_proj.1) | copy-start | bytes 393220
  2.2 9.4 %copy-start.8 = (f32[256]{0:T(256)S(1)}, f32[256]{0:T(256)}, u32[]{:S(2)}) copy-start(f32[256]{0:T(256)} %param.11) | copy-start | bytes 3076
  2.2 9.4 %copy-start.9 = (f32[256]{0:T(256)S(1)}, f32[256]{0:T(256)}, u32[]{:S(2)}) copy-start(f32[256]{0:T(256)} %param.15) | copy-start | bytes 3076

commit v4 on v3

--- a/solution.py
+++ b/solution.py
@@ -43,7 +43,7 @@
         strips[:, place, :] = found[place * heads : (place + 1) * heads]
 
 
-def halo_kernel(fields, rel_bias, north, east, corner, strips, padded, send_sems, recv_sems):
+def halo_kernel(fields, north, east, corner, send_sems, recv_sems):
     lat_half, lon_half = WIN_LAT // 2, WIN_LON // 2
     lat, lon = lax.axis_index("lat"), lax.axis_index("lon")
     lat_size, lon_size = lax.axis_size("lat"), lax.axis_size("lon")
@@ -88,7 +88,6 @@
         pl.semaphore_wait(barrier, 1)
 
     to_west.start()
-    bias_strips(rel_bias, padded, strips, fields.shape[2])
     to_west.wait()
 
     @pl.when(lat > 0)
@@ -103,7 +102,8 @@
 
 
 def gather_kernel(
-    slots, mask_ref, where_ref, fields, north, east, corner, own, leaving, info, sems
+    slots, mask_ref, where_ref, rel_bias, fields, north, east, corner,
+    own, leaving, info, strips, padded, sems,
 ):
     lat_windows = mask_ref.shape[0]
     lon_windows = fields.shape[1] // WIN_LON
@@ -183,6 +183,8 @@
         return rank + ocean
 
     lax.fori_loop(0, lat_windows * lon_windows, start, jnp.int32(0))
+
+    bias_strips(rel_bias, padded, strips, fields.shape[2])
 
     def finish(window, carry):
         row, col = window // lon_windows, window % lon_windows
@@ -432,28 +434,24 @@
     )(info, own, leaving, strips, gain_one, w_qkv, w_proj, gain_two, w_up, w_down)
 
 
-def exchange_halos(fields, rel_bias):
+def exchange_halos(fields):
     lat_cells, lon_cells, levels, features = fields.shape
     lat_half, lon_half = WIN_LAT // 2, WIN_LON // 2
-    heads, length = rel_bias.shape
-    group = WIN_LON * levels
     return pl.pallas_call(
         halo_kernel,
         out_shape=[
             jax.ShapeDtypeStruct((lat_half, lon_cells, levels, features), fields.dtype),
             jax.ShapeDtypeStruct((lat_cells, lon_half, levels, features), fields.dtype),
             jax.ShapeDtypeStruct((lat_half, lon_half, levels, features), fields.dtype),
-            jax.ShapeDtypeStruct((heads, group, 2 * WIN_LAT * group), jnp.float32),
         ],
-        in_specs=[pl.BlockSpec(memory_space=pltpu.HBM), vmem()],
-        out_specs=[any_space()] * 3 + [vmem()],
-        scratch_shapes=[pltpu.VMEM((heads, (length + 255) // 128 * 128), jnp.float32)]
-        + [pltpu.SemaphoreType.DMA((3,))] * 2,
+        in_specs=[any_space()],
+        out_specs=[any_space()] * 3,
+        scratch_shapes=[pltpu.SemaphoreType.DMA((3,))] * 2,
         cost_estimate=cost(0, fields.size),
         compiler_params=pltpu.CompilerParams(
-            collective_id=0, has_side_effects=True, vmem_limit_bytes=4 * 2**20
+            collective_id=0, has_side_effects=True, vmem_limit_bytes=2**20
         ),
-    )(fields, rel_bias)
+    )(fields)
 
 
 def body(fields, ocean_mask, gain_one, w_qkv, rel_bias, w_proj, gain_two, w_up, w_down):
@@ -461,23 +459,29 @@
     lat_windows = lat_cells // WIN_LAT
     lon_windows = lon_cells // WIN_LON
     slots = (lat_windows - 1) * lon_windows // 2
-    north, east, corner, strips = exchange_halos(fields, rel_bias)
+    north, east, corner = exchange_halos(fields)
+    heads, length = rel_bias.shape
+    group = WIN_LON * levels
     where = jnp.reshape(lax.axis_index("lon"), (1,)).astype(jnp.int32)
     shape = (WIN_LAT, WIN_LON, levels, features)
     window_count = lat_windows * lon_windows
-    own, leaving, info = pl.pallas_call(
+    own, leaving, info, strips = pl.pallas_call(
         functools.partial(gather_kernel, slots),
         out_shape=[
             jax.ShapeDtypeStruct((slots,) + shape, fields.dtype),
             jax.ShapeDtypeStruct((slots,) + shape, fields.dtype),
             jax.ShapeDtypeStruct((2,), jnp.int32),
+            jax.ShapeDtypeStruct((heads, group, 2 * WIN_LAT * group), jnp.float32),
         ],
-        in_specs=[smem(), smem()] + [any_space()] * 4,
-        out_specs=[vmem(), vmem(), smem()],
-        scratch_shapes=[pltpu.SemaphoreType.DMA((window_count,))],
+        in_specs=[smem(), smem(), vmem()] + [any_space()] * 4,
+        out_specs=[vmem(), vmem(), smem(), vmem()],
+        scratch_shapes=[
+            pltpu.VMEM((heads, (length + 255) // 128 * 128), jnp.float32),
+            pltpu.SemaphoreType.DMA((window_count,)),
+        ],
         cost_estimate=cost(0, 4 * fields.size),
-        compiler_params=pltpu.CompilerParams(vmem_limit_bytes=3 * 2**20),
-    )(ocean_mask, where, fields, north, east, corner)
+        compiler_params=pltpu.CompilerParams(vmem_limit_bytes=6 * 2**20),
+    )(ocean_mask, where, rel_bias, fields, north, east, corner)
     finished, returned = run_windows(
         info, own, leaving, strips, gain_one.reshape(1, -1), w_qkv, w_proj,
         gain_two.reshape(1, -1), w_up, w_down,

time: 38.3 us -> 39 us (1.018)
  Pallas kernels: 35.5 us -> 36.3 us
    pallas_call x1, Pallas kernels: 3.25 us -> 4 us  [body(): pl.pallas_call(functools.partial(gather_kernel, slots), out_shape=[jax.Sh...]
where the time goes in v4:
time: 39 us; the launch traced here: 38.6 us
  Pallas kernels  36.3 us (93%)
  local copies, waits for them, and re-layouts  2.18 us (6%)
    pallas_call x1, Pallas kernels, run_windows(): pl.pallas_call(functools.partial(window_kernel, chunk), out_shape=[jax.Sh...  24.3 us
    pallas_call x1, Pallas kernels, exchange_halos(): pl.pallas_call(halo_kernel, out_shape=[jax.ShapeDtypeStruct((lat_half, lo...  5.98 us
    pallas_call x1, Pallas kernels, body(): pl.pallas_call(functools.partial(gather_kernel, slots), out_shape=[jax.Sh...  4 us
    unnamed x20, local copies, waits for them, and re-layouts  2.18 us
    pallas_call x1, Pallas kernels, body(): pl.pallas_call(place_kernel, out_shape=jax.ShapeDtypeStruct(fields.shape,...  1.96 us

profile of v4, /device:TPU:3, one launch (start us, length us, event | category | flops | bytes accessed | tf_op | source)
XLA Modules:
  0.0 38.6 jit_solution(9161590532579171870)
XLA Ops:
  0.0 0.0 copy-start.3
  0.0 0.0 copy-start
  0.0 1.4 %copy-done = bf16[48,32,2,256]{3,2,1,0:T(2,128)(2,1)S(1)} copy-done((bf16[48,32,2,256]{3,2,1,0:T(2,128)(2,1)S(1)}, bf16[48,32,2,256]{3,2,1,0:T(2,128)(2,1)}, u32[]{:S(2)}) %copy-start) | copy-done | bytes 1572888
  1.4 0.0 copy-start.1
  1.4 0.0 copy-start.8
  1.4 0.0 copy-start.9
  1.4 6.0 %shard_map.91 = (bf16[4,32,2,256]{3,2,1,0:T(2,128)(2,1)S(1)}, bf16[48,4,2,256]{3,2,1,0:T(2,128)(2,1)S(1)}, bf16[4,4,2,256]{3,2,1,0:T(2,128)(2,1)S(1)}) custom-call(bf16[48,32,2,256]{3,2,1,0:T(2,128)(2,1)S(1)} %copy-done), custom_call_target="tpu_custom_call" | custom-call | bytes 786432 | tf_op jit(solution)/shard_map/pallas_call | solution.py:440
  7.4 0.0 copy-done.3
  7.4 0.0 copy-done.1
  7.4 0.0 copy-start.2
  7.4 0.7 %copy-done.2 = f32[8,675]{1,0:T(8,128)S(1)} copy-done((f32[8,675]{1,0:T(8,128)S(1)}, f32[8,675]{1,0:T(8,128)}, u32[]{:S(2)}) %copy-start.2) | copy-done | bytes 21624
  8.2 0.0 copy-start.4
  8.2 0.0 copy-start.5
  8.2 0.0 copy-start.6
  8.2 0.0 copy-start.7
  8.2 4.0 %shard_map.92 = (bf16[10,8,8,2,256]{4,3,2,1,0:T(2,128)(2,1)S(1)}, bf16[10,8,8,2,256]{4,3,2,1,0:T(2,128)(2,1)S(1)}, s32[2]{0:T(128)S(1)}, f32[8,16,256]{2,1,0:T(8,128)S(1)}) custom-call(s32[6,32]{1,0:T(8,128)S(1)} %copy-done.3, s32[1]{0:T(128)} %bitcast.where_ref, f32[8,675]{1,0:T(8,128)S(1)} %copy-done.2, bf16[48,32,2,256]{3,2,1,0:T(2,128)(2,1)S(1)} %copy-done.1, ...), custom_call_target="tpu_custom_call" | custom-call | bytes 3145728 | tf_op jit(solution)/shard_map/pallas_call | solution.py:468
  12.2 0.0 copy-done.8
  12.2 0.0 copy-done.9
  12.2 0.0 copy-done.4
  12.2 0.0 copy-done.5
  12.2 0.0 copy-done.6
  12.2 0.0 copy-done.7
  12.3 24.3 %shard_map.93 = (bf16[10,8,8,2,256]{4,3,2,1,0:T(2,128)(2,1)S(1)}, bf16[10,8,8,2,256]{4,3,2,1,0:T(2,128)(2,1)S(1)}) custom-call(s32[2]{0:T(128)S(1)} %get-tuple-element.17.info, bf16[10,8,8,2,256]{4,3,2,1,0:T(2,128)(2,1)S(1)} %get-tuple-element.18.own, bf16[10,8,8,2,256]{4,3,2,1,0:T(2,128)(2,1)S(1)} %get-tuple-element.19.leaving, ...), custom_call_target="tpu_custom_call" | custom-call | flops 2348810240 | bytes 1310720 | tf_op jit(solution)/shard_map/pallas_call | solution.py:417
  36.6 2.0 %shard_map.94 = bf16[48,32,2,256]{3,2,1,0:T(2,128)(2,1)} custom-call(s32[6,32]{1,0:T(8,128)S(1)} %copy-done.3, s32[1]{0:T(128)} %bitcast.where_ref, s32[2]{0:T(128)S(1)} %get-tuple-element.17.info, bf16[10,8,8,2,256]{4,3,2,1,0:T(2,128)(2,1)S(1)} %get-tuple-element.21.finished, bf16[10,8,8,2,256]{4,3,2,1,0:T(2,128)(2,1)S(1)} %get-tuple-element.22.returned), custom_call_target="tpu_custom_call" | custom-call | bytes 3145728 | tf_op jit(solution)/shard_map/pallas_call | solution.py:489
Async XLA Ops:
  0.0 7.4 %copy-start.3 = (s32[6,32]{1,0:T(8,128)S(1)}, s32[6,32]{1,0:T(8,128)}, u32[]{:S(2)}) copy-start(s32[6,32]{1,0:T(8,128)} %mask_ref.3) | copy-start | bytes 2308
  0.0 1.4 %copy-start = (bf16[48,32,2,256]{3,2,1,0:T(2,128)(2,1)S(1)}, bf16[48,32,2,256]{3,2,1,0:T(2,128)(2,1)}, u32[]{:S(2)}) copy-start(bf16[48,32,2,256]{3,2,1,0:T(2,128)(2,1)} %fields.3) | copy-start | bytes 4718596
  1.4 6.0 %copy-start.1 = (bf16[48,32,2,256]{3,2,1,0:T(2,128)(2,1)S(1)}, bf16[48,32,2,256]{3,2,1,0:T(2,128)(2,1)}, u32[]{:S(2)}) copy-start(bf16[48,32,2,256]{3,2,1,0:T(2,128)(2,1)} %fields.3) | copy-start | bytes 4718596
  1.4 10.8 %copy-start.8 = (f32[256]{0:T(256)S(1)}, f32[256]{0:T(256)}, u32[]{:S(2)}) copy-start(f32[256]{0:T(256)} %param.11) | copy-start | bytes 3076
  1.4 10.8 %copy-start.9 = (f32[256]{0:T(256)S(1)}, f32[256]{0:T(256)}, u32[]{:S(2)}) copy-start(f32[256]{0:T(256)} %param.15) | copy-start | bytes 3076
  7.4 0.7 %copy-start.2 = (f32[8,675]{1,0:T(8,128)S(1)}, f32[8,675]{1,0:T(8,128)}, u32[]{:S(2)}) copy-start(f32[8,675]{1,0:T(8,128)} %rel_bias.1) | copy-start | bytes 64804
  8.2 4.0 %copy-start.4 = (bf16[256,1024]{1,0:T(8,128)(2,1)S(1)}, bf16[256,1024]{1,0:T(8,128)(2,1)}, u32[]{:S(2)}) copy-start(bf16[256,1024]{1,0:T(8,128)(2,1)} %w_up.1) | copy-start | bytes 1572868
  8.2 4.0 %copy-start.5 = (bf16[1024,256]{1,0:T(8,128)(2,1)S(1)}, bf16[1024,256]{1,0:T(8,128)(2,1)}, u32[]{:S(2)}) copy-start(bf16[1024,256]{1,0:T(8,128)(2,1)} %w_down.1) | copy-start | bytes 1572868
  8.2 4.1 %copy-start.6 = (bf16[256,768]{1,0:T(8,128)(2,1)S(1)}, bf16[256,768]{1,0:T(8,128)(2,1)}, u32[]{:S(2)}) copy-start(bf16[256,768]{1,0:T(8,128)(2,1)} %w_qkv.1) | copy-start | bytes 1179652
  8.2 4.1 %copy-start.7 = (bf16[256,256]{1,0:T(8,128)(2,1)S(1)}, bf16[256,256]{1,0:T(8,128)(2,1)}, u32[]{:S(2)}) copy-start(bf16[256,256]{1,0:T(8,128)(2,1)} %w_proj.1) | copy-start | bytes 393220
